TPU v7x, 32 devices: a whole 2x2x4 slice. The times are simulated.
32 devices in a mesh: grp: 2 (over y), seq: 4 (over z), head: 2 (over x), clip: 2 (over core).
Axes of the slice: x: 2, y: 2, z: 4, core: 2. Of those that a mesh axis runs over, the one named last changes fastest.
Arguments:
- query_states: bfloat16 [4, 2048, 1536], P(('grp', 'clip'), 'seq', 'head'), parts along dimension 0, may hold values from -64 to 64
- key_states: bfloat16 [4, 2048, 1536], P(('grp', 'clip'), 'seq', 'head'), parts along dimension 0, may hold values from -4 to 4
- value_states: bfloat16 [4, 2048, 1536], P(('grp', 'clip'), 'seq', 'head'), parts along dimension 0, may hold values from -5 to 5
- output_grad: bfloat16 [4, 2048, 3072], P(('grp', 'clip'), 'seq', 'head'), parts along dimension 0, may hold values from -48 to 48
- w_out: bfloat16 [1536, 3072], P('head'), may hold values from -0.15625 to 0.15625
- key_list: int32 [4, 8, 8], P(('grp', 'clip')), parts along dimension 0, may hold values from 0 to 7, as said below
- key_count: int32 [4, 8], P(('grp', 'clip')), parts along dimension 0, may hold values from 1 to 8, as said below
Outputs:
- query_grad: bfloat16 [4, 2048, 1536], P(('grp', 'clip'), 'seq', 'head'), parts along dimension 0
- key_grad: bfloat16 [4, 2048, 1536], P(('grp', 'clip'), 'seq', 'head'), parts along dimension 0
- value_grad: bfloat16 [4, 2048, 1536], P(('grp', 'clip'), 'seq', 'head'), parts along dimension 0
- grad_features: float32 [4, 12, 3], P(('grp', 'clip'), 'head'), parts along dimension 0
There are 2 independent parts, one for each index of `grp`. A program takes and returns all parts, laid end to end along the dimension named above; an argument that names none is the same for every part. Nothing has to cross between parts.
Inputs may be any that keep to these rules, and one draw needn't show every extreme that they name: Tile i lies in frame block i // 4 at place i % 4. For each clip and query tile i the first key_count entries of key_list are distinct key tiles in ascending order, among them i itself, each at a place within 2 of i's place, in i's frame block or in the other one; the remaining entries equal i. `key_count`: in every draw some query tile lists 8 key tiles.
All inputs are finite; a program needn't handle non-finite values.
Results may differ from a plain program's by a relative error of at most 0.035.
Values may be sent and summed in bfloat16 or wider, within the bound.
No kernel may reach another device: no remote copies, remote signals or barrier semaphores. Data moves between devices by JAX's collectives and lax.ppermute only.
A program may use at most 128 MiB of HBM per device.

v0:
```python
import functools
import math

import jax
import jax.numpy as jnp
from jax import lax
from jax.experimental import pallas as pl
from jax.experimental.pallas import tpu as pltpu
from jax.sharding import PartitionSpec as P


HD = 128
TILE = 256
STAT_ROWS = 16
SMALL_GRANT = 12 << 20
ATTEND_GRANT = 24 << 20
SMEM = pl.BlockSpec(memory_space=pltpu.SMEM)
VMEM = pl.BlockSpec(memory_space=pltpu.VMEM)
ANY = pl.BlockSpec(memory_space=pl.ANY)
HBM = pl.BlockSpec(memory_space=pltpu.HBM)
NT = (((1,), (1,)), ((), ()))
NN = (((1,), (0,)), ((), ()))
TN = (((0,), (0,)), ((), ()))


def mm(lhs, rhs, dims):
    return lax.dot_general(lhs, rhs, dims, preferred_element_type=jnp.float32)


def stage_kernel(slots, kinds, chunks, heads_ref, *refs):
    tensors = refs[:kinds]
    grad_ref = refs[kinds]
    outs = refs[kinds + 1 : -1]
    sems = refs[-1]
    copies = []
    for piece, chunk in enumerate(chunks):
        span = pl.ds(chunk * TILE, TILE)
        copies.append(
            pltpu.make_async_copy(grad_ref.at[span, :], outs[len(slots) + piece], sems.at[piece, kinds])
        )
    for index, slot in enumerate(slots):
        cols = pl.ds(pl.multiple_of(heads_ref[slot] * HD, HD), HD)
        for j, tensor in enumerate(tensors):
            copies.append(
                pltpu.make_async_copy(tensor.at[:, cols], outs[index].at[j], sems.at[index, j])
            )
    for copy in copies:
        copy.start()
    for copy in copies:
        copy.wait()


def stage(heads, tensors, grad, slots, chunks):
    rows = grad.shape[0]
    kinds = len(tensors)
    held = [pltpu.with_memory_space_constraint(arr, pltpu.HBM) for arr in (*tensors, grad)]
    outs = pl.pallas_call(
        functools.partial(stage_kernel, slots, kinds, chunks),
        out_shape=[pltpu.VMEM((kinds, rows, HD), grad.dtype)] * len(slots)
        + [pltpu.VMEM((TILE, grad.shape[1]), grad.dtype)] * len(chunks),
        in_specs=[SMEM] + [HBM] * (kinds + 1),
        out_specs=[VMEM] * (len(slots) + len(chunks)),
        scratch_shapes=[pltpu.SemaphoreType.DMA((max(len(slots), len(chunks)), kinds + 1))],
        compiler_params=pltpu.CompilerParams(vmem_limit_bytes=SMALL_GRANT),
        cost_estimate=pl.CostEstimate(
            flops=0,
            transcendentals=0,
            bytes_accessed=4 * (len(slots) * kinds * rows * HD + len(chunks) * TILE * grad.shape[1]),
        ),
        name="stage_inputs",
    )(heads, *held)
    return outs[: len(slots)], outs[len(slots) :]


def pack_kernel(slots, heads_ref, q_ref, k_ref, v_ref, *refs):
    outs = refs[len(refs) - slots :]
    chunks = len(refs) // slots - 1
    for slot, out in enumerate(outs):
        cols = pl.ds(pl.multiple_of(heads_ref[slot] * HD, HD), HD)
        out[0] = q_ref[:, cols]
        out[1] = k_ref[:, cols]
        out[2] = v_ref[:, cols]
        for chunk in range(chunks):
            out[3, chunk * TILE : (chunk + 1) * TILE, :] = refs[chunk * slots + slot][...]


def pack(heads, query, key, value, grads):
    rows = query.shape[0]
    slots = heads.shape[0]
    kinds = 4 if grads else 3
    return pl.pallas_call(
        functools.partial(pack_kernel, slots),
        out_shape=[jax.ShapeDtypeStruct((kinds, rows, HD), query.dtype)] * slots,
        in_specs=[SMEM, VMEM, VMEM, VMEM] + [VMEM] * len(grads),
        out_specs=[VMEM] * slots,
        compiler_params=pltpu.CompilerParams(vmem_limit_bytes=SMALL_GRANT),
        cost_estimate=pl.CostEstimate(
            flops=0, transcendentals=0, bytes_accessed=6 * (query.size + slots * rows * HD)
        ),
        name="pack_heads",
    )(heads, query, key, value, *grads)


def project_own_kernel(src_ref, grad_ref, w_ref, out):
    out[0] = mm(grad_ref[...], w_ref[...], NT)


def project_own(src, grads, w_out):
    rows, feats = grads.shape
    width = w_out.shape[0]
    steps = width // (2 * HD)
    return pl.pallas_call(
        project_own_kernel,
        out_shape=jax.ShapeDtypeStruct((steps, rows, 2 * HD), jnp.float32),
        grid_spec=pltpu.PrefetchScalarGridSpec(
            num_scalar_prefetch=1,
            grid=(steps,),
            in_specs=[
                pl.BlockSpec((rows, feats), lambda s, src: (0, 0)),
                pl.BlockSpec((2 * HD, feats), lambda s, src: (s, src[0])),
            ],
            out_specs=pl.BlockSpec((1, rows, 2 * HD), lambda s, src: (s, 0, 0)),
        ),
        compiler_params=pltpu.CompilerParams(vmem_limit_bytes=SMALL_GRANT),
        cost_estimate=pl.CostEstimate(
            flops=2 * rows * feats * width,
            transcendentals=0,
            bytes_accessed=2 * (grads.size + width * feats) + 4 * rows * width,
        ),
        name="project_own",
    )(src, grads, w_out)


def project_rest_kernel(heads_ref, src_ref, grad_ref, w_ref, acc_ref, *refs):
    outs, held = refs[:-1], refs[-1]
    total = mm(grad_ref[...], w_ref[...], NT) + acc_ref[0]
    step = pl.program_id(0)
    for half in range(2):
        held[2 * step + half] = total[:, half * HD : (half + 1) * HD].astype(jnp.bfloat16)

    @pl.when(step == pl.num_programs(0) - 1)
    def _():
        for slot, out in enumerate(outs):
            out[...] = held[heads_ref[slot]]


def project_rest(heads, src, grads, w_out, acc, chunk):
    rows, feats = grads.shape
    slots = heads.shape[0]
    width = w_out.shape[0]
    steps = width // (2 * HD)
    return pl.pallas_call(
        project_rest_kernel,
        out_shape=[jax.ShapeDtypeStruct((rows, HD), jnp.bfloat16)] * slots,
        grid_spec=pltpu.PrefetchScalarGridSpec(
            num_scalar_prefetch=2,
            grid=(steps,),
            in_specs=[
                pl.BlockSpec((rows, feats), lambda s, heads, src: (0, 0)),
                pl.BlockSpec((2 * HD, feats), lambda s, heads, src: (s, src[0])),
                pl.BlockSpec((1, rows, 2 * HD), lambda s, heads, src: (s, chunk, 0)),
            ],
            out_specs=[pl.BlockSpec((rows, HD), lambda s, heads, src: (0, 0))] * slots,
            scratch_shapes=[pltpu.VMEM((width // HD, rows, HD), jnp.bfloat16)],
        ),
        compiler_params=pltpu.CompilerParams(vmem_limit_bytes=SMALL_GRANT),
        cost_estimate=pl.CostEstimate(
            flops=2 * rows * feats * width,
            transcendentals=0,
            bytes_accessed=2 * (grads.size + width * feats) + 6 * rows * width,
        ),
        name="project_rest",
    )(heads, src, grads, w_out, acc)


def attend_kernel(parts, tiles_dev, me_ref, mask_ref, *refs):
    @pl.when(me_ref[1] != 0)
    def _():
        attend_body(parts, tiles_dev, me_ref, mask_ref, *refs)


def attend_body(parts, tiles_dev, me_ref, mask_ref, *refs):
    tiles = parts * tiles_dev
    rows = tiles_dev * TILE
    blocks = refs[:parts]
    chunks = refs[parts : len(refs) - parts - 14]
    outs = refs[len(refs) - parts - 14 : len(refs) - 14]
    q_s, k_s, v_s, g_s, dk_s, dv_s, dq_s, e_s, dp_s, ds_s, m_s, l_s, d_s, sems = refs[-14:]
    score_scale = HD ** (-0.5)
    expo = score_scale * math.log2(math.e)
    me = me_ref[0]
    copies = []
    for part in range(parts):
        span = pl.ds(part * rows, rows)
        pairs = [(blocks[part].at[j], held.at[span]) for j, held in enumerate((q_s, k_s, v_s))]
        if chunks:
            for sub in range(tiles_dev):
                span = pl.ds(part * rows + sub * TILE, TILE)
                pairs.append((chunks[sub * parts + part], g_s.at[span]))
        else:
            pairs.append((blocks[part].at[3], g_s.at[span]))
        for j, (source, held) in enumerate(pairs):
            copies.append(pltpu.make_async_copy(source, held, sems.at[part, j]))
    for copy in copies:
        copy.start()
    for copy in copies:
        copy.wait()
    dk_s[...] = jnp.zeros_like(dk_s)
    dv_s[...] = jnp.zeros_like(dv_s)

    def home(part):
        return lax.rem(me - part + parts, parts) * tiles_dev

    def query_step(part, query_sq):
        own = home(part)
        span = pl.ds(pl.multiple_of(part * rows, rows), rows)
        query = q_s[span, :]
        grad = g_s[span, :]
        for ki in range(tiles):
            place = home(ki // tiles_dev) + ki % tiles_dev
            scores = mm(k_s[ki * TILE : (ki + 1) * TILE, :], query, NT)
            dprob = mm(v_s[ki * TILE : (ki + 1) * TILE, :], grad, NT)
            top = jnp.max(scores, axis=0, keepdims=True)
            weight = jnp.exp2((scores - top) * expo)
            for sub in range(tiles_dev):
                cols = slice(sub * TILE, (sub + 1) * TILE)
                live = mask_ref[own + sub, place] != 0
                m_s[ki : ki + 1, cols] = jnp.where(live, top[:, cols], -jnp.inf)
            l_s[ki : ki + 1, :] = jnp.sum(weight, axis=0, keepdims=True)
            d_s[ki : ki + 1, :] = jnp.sum(weight * dprob, axis=0, keepdims=True)
            e_s[ki] = weight
            dp_s[ki] = dprob

        tops = m_s[...]
        factor = jnp.exp2((tops - jnp.max(tops, axis=0, keepdims=True)) * expo)
        norm = jnp.sum(l_s[...] * factor, axis=0, keepdims=True)
        delta = jnp.sum(d_s[...] * factor, axis=0, keepdims=True) / norm
        m_s[...] = factor / norm
        for ki in range(tiles):
            weight = e_s[ki] * m_s[ki : ki + 1, :]
            dscore = (weight * (dp_s[ki] - delta)).astype(jnp.bfloat16)
            dv_s[ki] += mm(weight.astype(jnp.bfloat16), grad, NN)
            dk_s[ki] += mm(dscore, query, NN)
            ds_s[ki * TILE : (ki + 1) * TILE, :] = dscore

        query_full = mm(ds_s[...], k_s[...], TN) * score_scale
        dq_s[part] = query_full.astype(jnp.bfloat16)
        return query_sq + jnp.sum(query_full * query_full, axis=0, keepdims=True)

    query_sq = lax.fori_loop(0, parts, query_step, jnp.zeros((1, HD), jnp.float32))
    key_sq = jnp.zeros((1, HD), jnp.float32)
    value_sq = jnp.zeros((1, HD), jnp.float32)
    for part in range(parts):
        for sub in range(tiles_dev):
            tile = part * tiles_dev + sub
            key_full = dk_s[tile] * score_scale
            value_full = dv_s[tile]
            key_sq = key_sq + jnp.sum(key_full * key_full, axis=0, keepdims=True)
            value_sq = value_sq + jnp.sum(value_full * value_full, axis=0, keepdims=True)
            low = sub * TILE
            outs[part][low : low + TILE, :] = dq_s[part, low : low + TILE, :]
            outs[part][rows + low : rows + low + TILE, :] = key_full.astype(jnp.bfloat16)
            outs[part][2 * rows + low : 2 * rows + low + TILE, :] = value_full.astype(jnp.bfloat16)
    row = lax.broadcasted_iota(jnp.int32, (STAT_ROWS, HD), 0)
    total = jnp.where(
        row < 3,
        jnp.sum(query_sq, axis=1, keepdims=True),
        jnp.where(
            row < 6,
            jnp.sum(key_sq, axis=1, keepdims=True),
            jnp.sum(value_sq, axis=1, keepdims=True),
        ),
    )
    high = total.astype(jnp.bfloat16).astype(jnp.float32)
    mid = (total - high).astype(jnp.bfloat16).astype(jnp.float32)
    low = total - high - mid
    piece = lax.rem(row, 3)
    stats = jnp.where(piece == 0, high, jnp.where(piece == 1, mid, low)).astype(jnp.bfloat16)
    for part in range(parts):
        outs[part][3 * rows :, :] = stats


def attend(me, mask, blocks, chunks):
    parts = len(blocks)
    rows = blocks[0].shape[1]
    tiles_dev = rows // TILE
    tiles = parts * tiles_dev
    bf16, f32 = jnp.bfloat16, jnp.float32
    pairs = tiles * tiles
    return pl.pallas_call(
        functools.partial(attend_kernel, parts, tiles_dev),
        out_shape=[jax.ShapeDtypeStruct((3 * rows + STAT_ROWS, HD), bf16)] * parts,
        in_specs=[SMEM, SMEM] + [ANY] * (parts + len(chunks)),
        out_specs=[VMEM] * parts,
        scratch_shapes=[
            pltpu.VMEM((parts * rows, HD), bf16),
            pltpu.VMEM((parts * rows, HD), bf16),
            pltpu.VMEM((parts * rows, HD), bf16),
            pltpu.VMEM((parts * rows, HD), bf16),
            pltpu.VMEM((tiles, TILE, HD), f32),
            pltpu.VMEM((tiles, TILE, HD), f32),
            pltpu.VMEM((parts, rows, HD), bf16),
            pltpu.VMEM((tiles, TILE, rows), f32),
            pltpu.VMEM((tiles, TILE, rows), f32),
            pltpu.VMEM((tiles * TILE, rows), bf16),
            pltpu.VMEM((tiles, rows), f32),
            pltpu.VMEM((tiles, rows), f32),
            pltpu.VMEM((tiles, rows), f32),
            pltpu.SemaphoreType.DMA((parts, 3 + tiles_dev)),
        ],
        cost_estimate=pl.CostEstimate(
            flops=pairs * 10 * TILE * TILE * HD,
            transcendentals=pairs * TILE * TILE,
            bytes_accessed=2 * 7 * parts * rows * HD,
        ),
        compiler_params=pltpu.CompilerParams(vmem_limit_bytes=ATTEND_GRANT),
        name="attend_head",
    )(me, mask, *blocks, *chunks)


def unpack_kernel(parts, rows, count, fresh, heads_ref, live_ref, *refs):
    blocks = refs[:parts]
    rest = refs[parts:]
    feats = None
    if not fresh:
        feats = rest[3][...]
        rest = rest[4:]
    outs = rest[:3]
    feat_out = rest[3]
    sems = rest[4]
    if fresh:
        feats = jnp.zeros(feat_out.shape, jnp.float32)

    def copies(slot):
        cols = pl.ds(pl.multiple_of(heads_ref[slot] * HD, HD), HD)
        return [
            pltpu.make_async_copy(
                blocks[slot].at[pl.ds(j * rows, rows), :], outs[j].at[:, cols], sems.at[slot, j]
            )
            for j in range(3)
        ]

    for slot in range(parts):
        @pl.when(live_ref[slot] != 0)
        def _():
            for copy in copies(slot):
                copy.start()

    row = lax.broadcasted_iota(jnp.int32, feat_out.shape, 2)
    col = lax.broadcasted_iota(jnp.int32, feat_out.shape, 0)
    for slot in range(parts):
        stats = blocks[slot][3 * rows :, :].astype(jnp.float32)
        here = (row == heads_ref[slot]) & (live_ref[slot] != 0)
        for j in range(3):
            total = stats[3 * j : 3 * j + 1, :] + stats[3 * j + 1 : 3 * j + 2, :]
            total = total + stats[3 * j + 2 : 3 * j + 3, :]
            value = jnp.log(total / count + 1e-06)[:, : feat_out.shape[2]]
            feats = jnp.where(here & (col == j), value[None], feats)
    feat_out[...] = feats
    for slot in range(parts):
        @pl.when(live_ref[slot] != 0)
        def _():
            for copy in copies(slot):
                copy.wait()


def unpack(heads, live, blocks, before, head_count, count):
    parts = len(blocks)
    rows = (blocks[0].shape[0] - STAT_ROWS) // 3
    fresh = before is None
    kept = [] if fresh else list(before)
    big = jax.ShapeDtypeStruct((rows, head_count * HD), jnp.bfloat16)
    return pl.pallas_call(
        functools.partial(unpack_kernel, parts, rows, count, fresh),
        out_shape=[big, big, big, jax.ShapeDtypeStruct((3, 1, head_count), jnp.float32)],
        in_specs=[SMEM, SMEM] + [VMEM] * parts + ([] if fresh else [ANY, ANY, ANY, VMEM]),
        out_specs=[ANY, ANY, ANY, VMEM],
        scratch_shapes=[pltpu.SemaphoreType.DMA((parts, 3))],
        input_output_aliases={} if fresh else {2 + parts + j: j for j in range(3)},
        compiler_params=pltpu.CompilerParams(vmem_limit_bytes=SMALL_GRANT),
        cost_estimate=pl.CostEstimate(
            flops=0, transcendentals=0, bytes_accessed=12 * parts * rows * HD
        ),
        name="unpack_heads",
    )(heads, live, *blocks, *kept)


def shift(arr, axis, step, size, targets):
    pairs = [(s, (s + step) % size) for s in range(size) if (s + step) % size in targets]
    return lax.ppermute(arr, axis, pairs)


def shift_back(arr, axis, step, size, sources):
    return lax.ppermute(arr, axis, [(s, (s - step) % size) for s in sources])


def allowed_tiles(key_list, key_count):
    tiles, slots = key_list.shape
    live = jnp.arange(slots)[None, :] < key_count[:, None]
    hit = (key_list[:, :, None] == jnp.arange(tiles)[None, None, :]) & live[:, :, None]
    return jnp.any(hit, axis=1).astype(jnp.int32)


def by_heads(query_states, key_states, value_states, output_grad, w_out, key_list, key_count):
    parts = lax.axis_size("seq")
    me = lax.axis_index("seq")
    side = lax.axis_index("head")
    rows, width = query_states.shape[1:]
    head_count = width // HD
    full, extra = divmod(head_count, parts)
    low = (parts - extra) // 2
    rounds = [(k * parts, 0, parts) for k in range(full)]
    if extra:
        rounds.append((full * parts, low, extra))
    dest = lax.rem(me + jnp.arange(parts, dtype=jnp.int32), parts)
    heads, lives, targets = [], [], []
    for base, first, size in rounds:
        heads.append(base + jnp.clip(dest - first, 0, size - 1).astype(jnp.int32))
        lives.append(((dest >= first) & (dest < first + size)).astype(jnp.int32))
        targets.append(list(range(first, first + size)))
    mask = allowed_tiles(key_list[0], key_count[0])
    all_heads = jnp.concatenate(heads)
    chunk_count = rows // TILE
    tensors = (query_states[0], key_states[0], value_states[0])
    first, pieces = stage(heads[0], tensors, output_grad[0], range(1, parts), [0])
    own, rest = stage(heads[0], tensors, output_grad[0], [0], range(1, chunk_count))
    pieces = [*pieces, *rest]
    other = []
    for piece in pieces:
        if other:
            piece, _ = lax.optimization_barrier((piece, other[-1]))
        other.append(lax.ppermute(piece, "head", [(0, 1), (1, 0)]))
    side = side.astype(jnp.int32).reshape(1)
    blocks = [*own] + [shift(first[i - 1], "seq", i, parts, targets[0]) for i in range(1, parts)]
    acc = project_own(side, output_grad[0], w_out)
    projected = [
        project_rest(all_heads, 1 - side, other[chunk], w_out, acc, chunk)
        for chunk in range(chunk_count)
    ]
    chunks = []
    for slots in projected:
        chunks += [slots[0]]
        for i in range(1, parts):
            chunks += [shift(slots[i], "seq", i, parts, targets[0])]
    before = None
    for k in range(len(rounds)):
        me_live = jnp.stack([me.astype(jnp.int32), lives[k][0]])
        done = attend(me_live, mask, blocks, chunks)
        if k + 1 < len(rounds):
            grads = [slot for slots in projected for slot in slots[(k + 1) * parts : (k + 2) * parts]]
            slots = pack(heads[k + 1], *tensors, grads)
            blocks = [slots[0]]
            for i in range(1, parts):
                blocks += [shift(slots[i], "seq", i, parts, targets[k + 1])]
            chunks = []
        back = [done[0]] + [
            shift_back(done[i], "seq", i, parts, targets[k]) for i in range(1, parts)
        ]
        before = unpack(heads[k], lives[k], back, before, head_count, parts * rows * HD)
    query_grad, key_grad, value_grad, feats = before
    return query_grad[None], key_grad[None], value_grad[None], feats.transpose(1, 2, 0)


def attend_gathered(query_tiles, key_buf, value_buf, grad_tiles, buf_slots, counts):
    score_scale = HD ** (-0.5)
    tile_count, tile_rows, feat_width = query_tiles.shape
    slot_count = buf_slots.shape[1]
    key_span = slot_count * tile_rows
    buf_tiles = key_buf.shape[0]
    key_sel = key_buf[buf_slots].reshape(tile_count, key_span, feat_width)
    value_sel = value_buf[buf_slots].reshape(tile_count, key_span, feat_width)
    allowed = jnp.arange(key_span)[None, :] // tile_rows < counts[:, None]

    def head_step(head_idx, carried):
        query_acc, key_acc, value_acc = carried
        col_start = head_idx * HD
        query_head = lax.dynamic_slice_in_dim(query_tiles, col_start, HD, 2)
        key_head = lax.dynamic_slice_in_dim(key_sel, col_start, HD, 2)
        value_head = lax.dynamic_slice_in_dim(value_sel, col_start, HD, 2)
        grad_head = lax.dynamic_slice_in_dim(grad_tiles, col_start, HD, 2)
        scores = (
            jnp.einsum("iqe,ike->iqk", query_head, key_head, preferred_element_type=jnp.float32)
            * score_scale
        )
        scores = jnp.where(allowed[:, None, :], scores, -jnp.inf)
        row_max = jnp.max(scores, axis=-1, keepdims=True)
        log_norm = row_max + jnp.log(jnp.sum(jnp.exp(scores - row_max), axis=-1, keepdims=True))
        weights = jnp.exp(scores - log_norm)
        weights_b = weights.astype(jnp.bfloat16)
        attn_out = jnp.einsum(
            "iqk,ike->iqe", weights_b, value_head, preferred_element_type=jnp.float32
        ).astype(jnp.bfloat16)
        row_delta = jnp.sum(
            grad_head.astype(jnp.float32) * attn_out.astype(jnp.float32), axis=-1, keepdims=True
        )
        dprob = jnp.einsum(
            "iqe,ike->iqk", grad_head, value_head, preferred_element_type=jnp.float32
        )
        dscore = (weights * (dprob - row_delta)).astype(jnp.bfloat16)
        query_head_grad = score_scale * jnp.einsum(
            "iqk,ike->iqe", dscore, key_head, preferred_element_type=jnp.float32
        )
        key_head_grad = score_scale * jnp.einsum(
            "iqk,iqe->ike", dscore, query_head, preferred_element_type=jnp.float32
        )
        value_head_grad = jnp.einsum(
            "iqk,iqe->ike", weights_b, grad_head, preferred_element_type=jnp.float32
        )
        query_acc = lax.dynamic_update_slice_in_dim(query_acc, query_head_grad, col_start, 2)
        key_acc = lax.dynamic_update_slice_in_dim(key_acc, key_head_grad, col_start, 2)
        value_acc = lax.dynamic_update_slice_in_dim(value_acc, value_head_grad, col_start, 2)
        return (query_acc, key_acc, value_acc)

    start_state = (
        jnp.zeros((tile_count, tile_rows, feat_width), jnp.float32),
        jnp.zeros((tile_count, key_span, feat_width), jnp.float32),
        jnp.zeros((tile_count, key_span, feat_width), jnp.float32),
    )
    query_full, key_sel_grad, value_sel_grad = lax.fori_loop(
        0, feat_width // HD, head_step, start_state
    )
    live_slot = jnp.arange(slot_count)[None, :] < counts[:, None]
    routing = (
        (buf_slots[:, :, None] == jnp.arange(buf_tiles)[None, None, :]) & live_slot[:, :, None]
    ).astype(jnp.float32)
    key_grad_buf = jnp.einsum(
        "imb,imr->br",
        routing,
        key_sel_grad.reshape(tile_count, slot_count, tile_rows * feat_width),
        precision=lax.Precision.HIGHEST,
    )
    value_grad_buf = jnp.einsum(
        "imb,imr->br",
        routing,
        value_sel_grad.reshape(tile_count, slot_count, tile_rows * feat_width),
        precision=lax.Precision.HIGHEST,
    )
    return (
        query_full,
        key_grad_buf.reshape(buf_tiles, tile_rows, feat_width),
        value_grad_buf.reshape(buf_tiles, tile_rows, feat_width),
    )


def head_squares(grads_full, head_count):
    rows = grads_full.reshape(-1, head_count, HD)
    return jnp.sum(rows * rows, axis=(0, 2))


def by_gather(query_states, key_states, value_states, output_grad, w_out, key_list, key_count):
    seq_count = lax.axis_size("seq")
    seq_index = lax.axis_index("seq")
    tok_rows = query_states.shape[1]
    feat_width = query_states.shape[2]
    head_count = feat_width // HD
    tile_count = tok_rows // TILE
    first_tile = seq_index * tile_count
    own_lists = lax.dynamic_slice_in_dim(key_list[0], first_tile, tile_count, 0)
    own_counts = lax.dynamic_slice_in_dim(key_count[0], first_tile, tile_count, 0)
    grad_out = lax.dot_general(
        lax.all_gather(output_grad, "head", axis=2, tiled=True)[0],
        w_out,
        (((1,), (1,)), ((), ())),
        preferred_element_type=jnp.float32,
    ).astype(jnp.bfloat16)
    query_tiles = query_states[0].reshape(tile_count, TILE, feat_width)
    grad_tiles = grad_out.reshape(tile_count, TILE, feat_width)
    key_whole, value_whole = (
        lax.all_gather(key_states, "seq", axis=1, tiled=True),
        lax.all_gather(value_states, "seq", axis=1, tiled=True),
    )
    key_buf = key_whole[0].reshape(-1, TILE, feat_width)
    value_buf = value_whole[0].reshape(-1, TILE, feat_width)
    query_full, key_grad_buf, value_grad_buf = attend_gathered(
        query_tiles, key_buf, value_buf, grad_tiles, own_lists, own_counts
    )
    buf_rows = key_grad_buf.shape[0] * TILE
    key_sum, value_sum = (
        lax.psum_scatter(
            key_grad_buf.reshape(1, buf_rows, feat_width).astype(jnp.bfloat16),
            "seq",
            scatter_dimension=1,
            tiled=True,
        ).astype(jnp.float32),
        lax.psum_scatter(
            value_grad_buf.reshape(1, buf_rows, feat_width).astype(jnp.bfloat16),
            "seq",
            scatter_dimension=1,
            tiled=True,
        ).astype(jnp.float32),
    )
    key_full = key_sum[0]
    value_full = value_sum[0]
    query_rows = query_full.reshape(tok_rows, feat_width)
    local_sums = jnp.stack(
        [
            head_squares(query_rows, head_count),
            head_squares(key_full, head_count),
            head_squares(value_full, head_count),
        ],
        axis=-1,
    )
    total_sums = lax.psum(local_sums, "seq")
    grad_features = jnp.log(total_sums / (seq_count * tok_rows * HD) + 1e-06)
    return (
        query_rows.astype(jnp.bfloat16)[None],
        key_full.astype(jnp.bfloat16)[None],
        value_full.astype(jnp.bfloat16)[None],
        grad_features[None],
    )


def per_device(*args):
    parts, sides = lax.axis_size("seq"), lax.axis_size("head")
    head_count = args[0].shape[2] // HD
    if head_count >= parts > 1 and head_count % 2 == 0 and sides == 2:
        return by_heads(*args)
    return by_gather(*args)


def solution(mesh):
    in_specs = (
        P(("grp", "clip"), "seq", "head"),
        P(("grp", "clip"), "seq", "head"),
        P(("grp", "clip"), "seq", "head"),
        P(("grp", "clip"), "seq", "head"),
        P("head", None),
        P(("grp", "clip"), None, None),
        P(("grp", "clip"), None),
    )
    out_specs = (
        P(("grp", "clip"), "seq", "head"),
        P(("grp", "clip"), "seq", "head"),
        P(("grp", "clip"), "seq", "head"),
        P(("grp", "clip"), "head", None),
    )
    return jax.shard_map(
        per_device, mesh=mesh, in_specs=in_specs, out_specs=out_specs, check_vma=False
    )
```

profile of v0, /device:TPU:4, one launch (start us, length us, event | category | flops | bytes accessed | tf_op | source)
XLA Modules:
  0.0 135.6 jit_solution(2842618253321115605)
XLA Ops:
  0.7 3.1 %stage_inputs.2 = (bf16[3,512,128]{2,1,0:T(8,128)(2,1)}, bf16[3,512,128]{2,1,0:T(8,128)(2,1)}, bf16[3,512,128]{2,1,0:T(8,128)(2,1)}, bf16[256,1536]{1,0:T(8,128)(2,1)S(1)}) custom-call(s32[4]{0:T(128)S(1)} %broadcast_clamp_fusion.heads_ref, bf16[512,768]{1,0:T(8,128)(2,1)} %bitcast.19, bf16[512,768]{1,0:T(8,128)(2,1)} %bitcast.22, ...), custom_call_target="tpu_custom_call" | custom-call | bytes 3932160 | tf_op jit(solution)/shard_map/stage_inputs/pallas_call | solution.py:57
  3.8 1.6 %collective-permute-start = (bf16[256,1536]{1,0:T(8,128)(2,1)S(1)}, bf16[256,1536]{1,0:T(8,128)(2,1)S(1)}, u32[]{:S(2)}, u32[]{:S(2)}) collective-permute-start(bf16[256,1536]{1,0:T(8,128)(2,1)S(1)} %get-tuple-element.47), channel_id=1, source_target_pairs={{0,2},{2,0},{1,3},{3,1},{4,6},{6,4},{5,7},{7,5},{8,10},{10,8},{9,1... | collective-permute-start | bytes 2359304 | tf_op jit(solution)/shard_map/ppermute | solution.py:432
  5.4 1.6 %collective-permute-start.8 = (bf16[3,512,128]{2,1,0:T(8,128)(2,1)}, bf16[3,512,128]{2,1,0:T(8,128)(2,1)S(1)}, u32[]{:S(2)}, u32[]{:S(2)}) collective-permute-start(bf16[3,512,128]{2,1,0:T(8,128)(2,1)} %get-tuple-element.67), channel_id=1, source_target_pairs={{0,4},{4,8},{8,12},{12,0},{1,5},{5,9},{9,13},{13,1},{2,6},{6,10},{... | collective-permute-start | bytes 1179656 | tf_op jit(solution)/shard_map/ppermute | solution.py:390
  6.9 2.6 %collective-permute-start.9 = (bf16[3,512,128]{2,1,0:T(8,128)(2,1)}, bf16[3,512,128]{2,1,0:T(8,128)(2,1)}, u32[]{:S(2)}, u32[]{:S(2)}) collective-permute-start(bf16[3,512,128]{2,1,0:T(8,128)(2,1)} %get-tuple-element.68), channel_id=1, source_target_pairs={{0,8},{4,12},{8,0},{12,4},{1,9},{5,13},{9,1},{13,5},{2,10},{6,14},... | collective-permute-start | bytes 1179656 | tf_op jit(solution)/shard_map/ppermute | solution.py:390
  9.5 1.3 collective-permute-start.10
  10.9 2.7 %stage_inputs.3 = (bf16[3,512,128]{2,1,0:T(8,128)(2,1)S(1)}, bf16[256,1536]{1,0:T(8,128)(2,1)}) custom-call(s32[4]{0:T(128)S(1)} %broadcast_clamp_fusion.heads_ref, bf16[512,768]{1,0:T(8,128)(2,1)} %bitcast.20, bf16[512,768]{1,0:T(8,128)(2,1)} %bitcast.23, bf16[512,768]{1,0:T(8,128)(2,1)} %bitcast.26, bf16[512,1536]{1,0:T(8,128)(2,1)} %bitcast.17), custom_call_target="tpu_custom_call" | custom-call | bytes 2359296 | tf_op jit(solution)/shard_map/stage_inputs/pallas_call | solution.py:57
  13.6 0.0 copy-start.5
  13.6 0.7 copy-done.5
  14.3 8.8 %collective-permute-done.grad_ref = bf16[256,1536]{1,0:T(8,128)(2,1)S(1)} collective-permute-done((bf16[256,1536]{1,0:T(8,128)(2,1)S(1)}, bf16[256,1536]{1,0:T(8,128)(2,1)S(1)}, u32[]{:S(2)}, u32[]{:S(2)}) %collective-permute-start) | collective-permute-done | bytes 786464 | tf_op jit(solution)/shard_map/ppermute | solution.py:432
  23.1 1.5 %collective-permute-start.1 = (bf16[256,1536]{1,0:T(8,128)(2,1)}, bf16[256,1536]{1,0:T(8,128)(2,1)}, u32[]{:S(2)}, u32[]{:S(2)}) collective-permute-start(bf16[256,1536]{1,0:T(8,128)(2,1)} %get-tuple-element.53), channel_id=1, source_target_pairs={{0,2},{2,0},{1,3},{3,1},{4,6},{6,4},{5,7},{7,5},{8,10},{10,8},{9,1... | collective-permute-start | bytes 2359304 | tf_op jit(solution)/shard_map/ppermute | solution.py:432
  24.6 0.0 copy-done.1
  24.6 0.0 copy-start
  24.7 2.3 %copy-done = bf16[768,3072]{1,0:T(8,128)(2,1)S(1)} copy-done((bf16[768,3072]{1,0:T(8,128)(2,1)S(1)}, bf16[768,3072]{1,0:T(8,128)(2,1)}, u32[]{:S(2)}) %copy-start) | copy-done | bytes 4718616
  27.0 2.0 %project_own.1.acc_ref = f32[3,512,256]{2,1,0:T(8,128)S(1)} custom-call(s32[1]{0:T(128)} %bitcast.6.src_ref, bf16[512,1536]{1,0:T(8,128)(2,1)S(1)} %bitcast.18, bf16[768,3072]{1,0:T(8,128)(2,1)S(1)} %copy-done), custom_call_target="tpu_custom_call" | custom-call | flops 1207959552 | bytes 5505024 | tf_op jit(solution)/shard_map/project_own/pallas_call | solution.py:112
  29.0 0.0 copy-done.8
  29.0 0.1 iota_compare_fusion.1
  29.1 0.1 pad_add_fusion.1.heads_ref
  29.2 0.1 fusion.1
  29.3 0.0 slice-done.1
  29.3 2.0 %project_rest.2 = (bf16[256,128]{1,0:T(8,128)(2,1)S(1)}, bf16[256,128]{1,0:T(8,128)(2,1)S(1)}, bf16[256,128]{1,0:T(8,128)(2,1)S(1)}, bf16[256,128]{1,0:T(8,128)(...) custom-call(s32[8]{0:T(128)S(1)} %pad_add_fusion.1.heads_ref, ...), custom_call_target="tpu_custom_call" | custom-call | flops 603979776 | bytes 4325376 | tf_op jit(solution)/shard_map/project_rest/pallas_call | solution.py:152
  31.4 1.6 %collective-permute-start.11 = (bf16[256,128]{1,0:T(8,128)(2,1)S(1)}, bf16[256,128]{1,0:T(8,128)(2,1)S(1)}, u32[]{:S(2)}, u32[]{:S(2)}) collective-permute-start(bf16[256,128]{1,0:T(8,128)(2,1)S(1)} %get-tuple-element.71), channel_id=1, source_target_pairs={{0,4},{4,8},{8,12},{12,0},{1,5},{5,9},{9,13},{13,1},{2,6},{6,10},{... | collective-permute-start | bytes 196616 | tf_op jit(solution)/shard_map/ppermute | solution.py:390
  33.0 9.0 %collective-permute-done.1.grad_ref = bf16[256,1536]{1,0:T(8,128)(2,1)} collective-permute-done((bf16[256,1536]{1,0:T(8,128)(2,1)}, bf16[256,1536]{1,0:T(8,128)(2,1)}, u32[]{:S(2)}, u32[]{:S(2)}) %collective-permute-start.1) | collective-permute-done | bytes 786464 | tf_op jit(solution)/shard_map/ppermute | solution.py:432
  42.0 2.6 %collective-permute-start.12 = (bf16[256,128]{1,0:T(8,128)(2,1)S(1)}, bf16[256,128]{1,0:T(8,128)(2,1)S(1)}, u32[]{:S(2)}, u32[]{:S(2)}) collective-permute-start(bf16[256,128]{1,0:T(8,128)(2,1)S(1)} %get-tuple-element.72), channel_id=1, source_target_pairs={{0,8},{4,12},{8,0},{12,4},{1,9},{5,13},{9,1},{13,5},{2,10},{6,14},... | collective-permute-start | bytes 196616 | tf_op jit(solution)/shard_map/ppermute | solution.py:390
  44.6 3.1 %project_rest.3 = (bf16[256,128]{1,0:T(8,128)(2,1)S(1)}, bf16[256,128]{1,0:T(8,128)(2,1)S(1)}, bf16[256,128]{1,0:T(8,128)(2,1)S(1)}, bf16[256,128]{1,0:T(8,128)(...) custom-call(s32[8]{0:T(128)S(1)} %pad_add_fusion.1.heads_ref, ...), custom_call_target="tpu_custom_call" | custom-call | flops 603979776 | bytes 4325376 | tf_op jit(solution)/shard_map/project_rest/pallas_call | solution.py:152
  47.7 0.0 collective-permute-done.8.refs_1_
  47.7 1.4 %collective-permute-start.13 = (bf16[256,128]{1,0:T(8,128)(2,1)S(1)}, bf16[256,128]{1,0:T(8,128)(2,1)S(1)}, u32[]{:S(2)}, u32[]{:S(2)}) collective-permute-start(bf16[256,128]{1,0:T(8,128)(2,1)S(1)} %get-tuple-element.73), channel_id=1, source_target_pairs={{0,12},{4,0},{8,4},{12,8},{1,13},{5,1},{9,5},{13,9},{2,14},{6,2},{... | collective-permute-start | bytes 196616 | tf_op jit(solution)/shard_map/ppermute | solution.py:390
  49.1 0.0 collective-permute-done.9.refs_2_
  49.1 0.7 collective-permute-start.14
  49.8 0.1 pad_add_fusion.me_ref
  49.9 0.0 copy-done.3
  49.9 0.8 pack_heads.1
  50.8 0.0 collective-permute-done.10.refs_3_
  50.8 1.0 collective-permute-start.15
  51.8 0.0 collective-permute-done.11.refs_5_
  51.8 2.9 %collective-permute-start.16 = (bf16[256,128]{1,0:T(8,128)(2,1)S(1)}, bf16[256,128]{1,0:T(8,128)(2,1)S(1)}, u32[]{:S(2)}, u32[]{:S(2)}) collective-permute-start(bf16[256,128]{1,0:T(8,128)(2,1)S(1)} %get-tuple-element.77), channel_id=1, source_target_pairs={{0,12},{4,0},{8,4},{12,8},{1,13},{5,1},{9,5},{13,9},{2,14},{6,2},{... | collective-permute-start | bytes 196616 | tf_op jit(solution)/shard_map/ppermute | solution.py:390
  54.7 0.0 collective-permute-done.12.refs_6_
  54.7 1.8 %collective-permute-start.2 = (bf16[4,512,128]{2,1,0:T(8,128)(2,1)S(1)}, bf16[4,512,128]{2,1,0:T(8,128)(2,1)S(1)}, u32[]{:S(2)}, u32[]{:S(2)}) collective-permute-start(bf16[4,512,128]{2,1,0:T(8,128)(2,1)S(1)} %get-tuple-element.59), channel_id=1, source_target_pairs={{0,4},{4,8},{1,5},{5,9},{2,6},{6,10},{3,7},{7,11},{16,20},{20,24},... | collective-permute-start | bytes 1572872 | tf_op jit(solution)/shard_map/ppermute | solution.py:390
  56.5 0.0 collective-permute-done.13.refs_7_
  56.5 2.7 %collective-permute-start.3 = (bf16[4,512,128]{2,1,0:T(8,128)(2,1)S(1)}, bf16[4,512,128]{2,1,0:T(8,128)(2,1)S(1)}, u32[]{:S(2)}, u32[]{:S(2)}) collective-permute-start(bf16[4,512,128]{2,1,0:T(8,128)(2,1)S(1)} %get-tuple-element.60), channel_id=1, source_target_pairs={{0,8},{12,4},{1,9},{13,5},{2,10},{14,6},{3,11},{15,7},{16,24},{28,... | collective-permute-start | bytes 1572872 | tf_op jit(solution)/shard_map/ppermute | solution.py:390
  59.3 0.0 collective-permute-done.14.refs_9_
  59.3 0.7 collective-permute-start.4
  60.0 0.1 pad_add_fusion.2.me_ref
  60.1 0.0 collective-permute-done.15.refs_10_
  60.1 0.0 collective-permute-done.16.refs_11_
  60.1 0.0 copy-done.6
  60.1 18.6 %attend_head.3 = (bf16[1552,128]{1,0:T(8,128)(2,1)S(1)}, bf16[1552,128]{1,0:T(8,128)(2,1)S(1)}, bf16[1552,128]{1,0:T(8,128)(2,1)S(1)}, bf16[1552,128]{1,0:T(8,128)(2,1)S(1)}) custom-call(s32[2]{0:T(128)S(1)} %pad_add_fusion.2.me_ref, s32[8,8]{1,0:T(8,128)S(1)} %convert_element_type.10.mask_ref, bf16[3,512,128]{2,1,0:T(8,128)(2,1)S(1)} %copy-done.6, ...), custom_call_target="tpu_custom_call" | custom-call | flops 5368709120 | bytes 3670016 | tf_op jit(solution)/shard_map/attend_head/pallas_call | solution.py:290
  78.8 4.2 %collective-permute-start.17 = (bf16[1552,128]{1,0:T(8,128)(2,1)S(1)}, bf16[1552,128]{1,0:T(8,128)(2,1)S(1)}, u32[]{:S(2)}, u32[]{:S(2)}) collective-permute-start(bf16[1552,128]{1,0:T(8,128)(2,1)S(1)} %get-tuple-element.79), channel_id=1, source_target_pairs={{0,12},{4,0},{8,4},{12,8},{1,13},{5,1},{9,5},{13,9},{2,14},{6,2},{... | collective-permute-start | bytes 1191944 | tf_op jit(solution)/shard_map/ppermute | solution.py:394
  83.0 0.0 collective-permute-start.18
  83.0 0.0 collective-permute-done.2.refs_1_
  83.0 1.1 collective-permute-start.19
  84.1 0.0 collective-permute-done.3.refs_2_
  84.1 0.0 collective-permute-done.4.refs_3_
  84.1 0.8 attend_head.2
  84.9 1.3 collective-permute-start.5
  86.2 1.3 collective-permute-start.6
  87.5 5.1 %collective-permute-done.17.refs_1_ = bf16[1552,128]{1,0:T(8,128)(2,1)S(1)} collective-permute-done((bf16[1552,128]{1,0:T(8,128)(2,1)S(1)}, bf16[1552,128]{1,0:T(8,128)(2,1)S(1)}, u32[]{:S(2)}, u32[]{:S(2)}) %collective-permute-start.17) | collective-permute-done | bytes 397344 | tf_op jit(solution)/shard_map/ppermute | solution.py:394
  92.6 0.7 collective-permute-start.7
  93.3 24.4 %collective-permute-done.18.refs_2_ = bf16[1552,128]{1,0:T(8,128)(2,1)S(1)} collective-permute-done((bf16[1552,128]{1,0:T(8,128)(2,1)S(1)}, bf16[1552,128]{1,0:T(8,128)(2,1)S(1)}, u32[]{:S(2)}, u32[]{:S(2)}) %collective-permute-start.18) | collective-permute-done | bytes 397344 | tf_op jit(solution)/shard_map/ppermute | solution.py:394
  117.7 0.0 collective-permute-done.19.refs_3_
  117.7 1.8 %unpack_heads.2 = (bf16[512,768]{1,0:T(8,128)(2,1)}, bf16[512,768]{1,0:T(8,128)(2,1)}, bf16[512,768]{1,0:T(8,128)(2,1)}, f32[3,1,6]{2,1,0:T(1,128)S(1)}) custom-call(s32[4]{0:T(128)S(1)} %broadcast_clamp_fusion.heads_ref, s32[4]{0:T(128)S(1)} %and_convert_fusion.live_ref, bf16[1552,128]{1,0:T(8,128)(2,1)S(1)} %get-tuple-element.78.refs_0_, ...), custom_call_target="tpu_custom_call" | custom-call | bytes 3145728 | tf_op jit(solution)/shard_map/unpack_heads/pallas_call | solution.py:373
  119.5 5.6 %collective-permute-done.5.refs_1_ = bf16[1552,128]{1,0:T(8,128)(2,1)S(1)} collective-permute-done((bf16[1552,128]{1,0:T(8,128)(2,1)S(1)}, bf16[1552,128]{1,0:T(8,128)(2,1)S(1)}, u32[]{:S(2)}, u32[]{:S(2)}) %collective-permute-start.5) | collective-permute-done | bytes 397344 | tf_op jit(solution)/shard_map/ppermute | solution.py:394
  125.0 8.5 %collective-permute-done.6.refs_2_ = bf16[1552,128]{1,0:T(8,128)(2,1)S(1)} collective-permute-done((bf16[1552,128]{1,0:T(8,128)(2,1)S(1)}, bf16[1552,128]{1,0:T(8,128)(2,1)S(1)}, u32[]{:S(2)}, u32[]{:S(2)}) %collective-permute-start.6) | collective-permute-done | bytes 397344 | tf_op jit(solution)/shard_map/ppermute | solution.py:394
  133.5 0.0 collective-permute-done.7.refs_3_
  133.5 2.1 %unpack_heads.3 = (bf16[512,768]{1,0:T(8,128)(2,1)}, bf16[512,768]{1,0:T(8,128)(2,1)}, bf16[512,768]{1,0:T(8,128)(2,1)}, f32[3,1,6]{2,1,0:T(1,128)}) custom-call(s32[4]{0:T(128)S(1)} %clamp_add_fusion.heads_ref, s32[4]{0:T(128)S(1)} %and_convert_fusion.1.live_ref, ...), custom_call_target="tpu_custom_call", output_to_operand_aliasing={{0}: (6, {}), {1}: (7, {}), {2}: (8, {})} | custom-call | bytes 3145728 | tf_op jit(solution)/shard_map/unpack_heads/pallas_call | solution.py:373
  (19 shorter events, 0.1 us)
Async XLA Ops:
  3.8 19.3 %collective-permute-start = (bf16[256,1536]{1,0:T(8,128)(2,1)S(1)}, bf16[256,1536]{1,0:T(8,128)(2,1)S(1)}, u32[]{:S(2)}, u32[]{:S(2)}) collective-permute-start(bf16[256,1536]{1,0:T(8,128)(2,1)S(1)} %get-tuple-element.47), channel_id=1, source_target_pairs={{0,2},{2,0},{1,3},{3,1},{4,6},{6,4},{5,7},{7,5},{8,10},{10,8},{9,1... | collective-permute-start | bytes 2359304 | tf_op jit(solution)/shard_map/ppermute | solution.py:432
  5.4 42.4 %collective-permute-start.8 = (bf16[3,512,128]{2,1,0:T(8,128)(2,1)}, bf16[3,512,128]{2,1,0:T(8,128)(2,1)S(1)}, u32[]{:S(2)}, u32[]{:S(2)}) collective-permute-start(bf16[3,512,128]{2,1,0:T(8,128)(2,1)} %get-tuple-element.67), channel_id=1, source_target_pairs={{0,4},{4,8},{8,12},{12,0},{1,5},{5,9},{9,13},{13,1},{2,6},{6,10},{... | collective-permute-start | bytes 1179656 | tf_op jit(solution)/shard_map/ppermute | solution.py:390
  6.9 42.2 %collective-permute-start.9 = (bf16[3,512,128]{2,1,0:T(8,128)(2,1)}, bf16[3,512,128]{2,1,0:T(8,128)(2,1)}, u32[]{:S(2)}, u32[]{:S(2)}) collective-permute-start(bf16[3,512,128]{2,1,0:T(8,128)(2,1)} %get-tuple-element.68), channel_id=1, source_target_pairs={{0,8},{4,12},{8,0},{12,4},{1,9},{5,13},{9,1},{13,5},{2,10},{6,14},... | collective-permute-start | bytes 1179656 | tf_op jit(solution)/shard_map/ppermute | solution.py:390
  9.5 15.1 %copy-start.1 = (bf16[1,512,1536]{2,1,0:T(8,128)(2,1)S(1)}, bf16[1,512,1536]{2,1,0:T(8,128)(2,1)}, u32[]{:S(2)}) copy-start(bf16[1,512,1536]{2,1,0:T(8,128)(2,1)} %param.10) | copy-start | bytes 4718596
  9.5 41.3 %collective-permute-start.10 = (bf16[3,512,128]{2,1,0:T(8,128)(2,1)}, bf16[3,512,128]{2,1,0:T(8,128)(2,1)}, u32[]{:S(2)}, u32[]{:S(2)}) collective-permute-start(bf16[3,512,128]{2,1,0:T(8,128)(2,1)} %get-tuple-element.69), channel_id=1, source_target_pairs={{0,12},{4,0},{8,4},{12,8},{1,13},{5,1},{9,5},{13,9},{2,14},{6,2},{... | collective-permute-start | bytes 1179656 | tf_op jit(solution)/shard_map/ppermute | solution.py:390
  10.9 18.4 %slice-start = ((s8[4718592]{0:T(1024)(128)(4,1)}), s8[524288]{0:T(1024)(128)(4,1)S(1)}, s32[]{:S(2)}) async-start(s8[4718592]{0:T(1024)(128)(4,1)} %bitcast.14), calls=%async_computation | async-start | bytes 1048576
  13.6 0.7 copy-start.5
  23.1 18.8 %collective-permute-start.1 = (bf16[256,1536]{1,0:T(8,128)(2,1)}, bf16[256,1536]{1,0:T(8,128)(2,1)}, u32[]{:S(2)}, u32[]{:S(2)}) collective-permute-start(bf16[256,1536]{1,0:T(8,128)(2,1)} %get-tuple-element.53), channel_id=1, source_target_pairs={{0,2},{2,0},{1,3},{3,1},{4,6},{6,4},{5,7},{7,5},{8,10},{10,8},{9,1... | collective-permute-start | bytes 2359304 | tf_op jit(solution)/shard_map/ppermute | solution.py:432
  24.6 2.3 %copy-start = (bf16[768,3072]{1,0:T(8,128)(2,1)S(1)}, bf16[768,3072]{1,0:T(8,128)(2,1)}, u32[]{:S(2)}) copy-start(bf16[768,3072]{1,0:T(8,128)(2,1)} %w_ref.5) | copy-start | bytes 14155780
  27.0 2.0 %copy-start.8 = (s32[1,8]{1,0:T(1,128)S(1)}, s32[1,8]{1,0:T(1,128)}, u32[]{:S(2)}) copy-start(s32[1,8]{1,0:T(1,128)} %param.13) | copy-start | bytes 100
  27.0 2.2 %copy-start.7 = (s32[1,8,8]{2,1,0:T(8,128)S(1)}, s32[1,8,8]{2,1,0:T(8,128)}, u32[]{:S(2)}) copy-start(s32[1,8,8]{2,1,0:T(8,128)} %param.12) | copy-start | bytes 772
  27.0 2.3 %slice-start.1 = ((s8[4718592]{0:T(1024)(128)(4,1)}), s8[4194304]{0:T(1024)(128)(4,1)S(1)}, s32[]{:S(2)}) async-start(s8[4718592]{0:T(1024)(128)(4,1)} %bitcast.14), calls=%async_computation.1 | async-start | bytes 8388608
  31.4 20.4 %collective-permute-start.11 = (bf16[256,128]{1,0:T(8,128)(2,1)S(1)}, bf16[256,128]{1,0:T(8,128)(2,1)S(1)}, u32[]{:S(2)}, u32[]{:S(2)}) collective-permute-start(bf16[256,128]{1,0:T(8,128)(2,1)S(1)} %get-tuple-element.71), channel_id=1, source_target_pairs={{0,4},{4,8},{8,12},{12,0},{1,5},{5,9},{9,13},{13,1},{2,6},{6,10},{... | collective-permute-start | bytes 196616 | tf_op jit(solution)/shard_map/ppermute | solution.py:390
  42.0 7.9 %copy-start.2 = (bf16[1,512,768]{2,1,0:T(8,128)(2,1)S(1)}, bf16[1,512,768]{2,1,0:T(8,128)(2,1)}, u32[]{:S(2)}) copy-start(bf16[1,512,768]{2,1,0:T(8,128)(2,1)} %param.7) | copy-start | bytes 2359300
  42.0 7.9 %copy-start.3 = (bf16[1,512,768]{2,1,0:T(8,128)(2,1)S(1)}, bf16[1,512,768]{2,1,0:T(8,128)(2,1)}, u32[]{:S(2)}) copy-start(bf16[1,512,768]{2,1,0:T(8,128)(2,1)} %param.8) | copy-start | bytes 2359300
  42.0 7.9 %copy-start.4 = (bf16[1,512,768]{2,1,0:T(8,128)(2,1)S(1)}, bf16[1,512,768]{2,1,0:T(8,128)(2,1)}, u32[]{:S(2)}) copy-start(bf16[1,512,768]{2,1,0:T(8,128)(2,1)} %param.9) | copy-start | bytes 2359300
  42.0 12.7 %collective-permute-start.12 = (bf16[256,128]{1,0:T(8,128)(2,1)S(1)}, bf16[256,128]{1,0:T(8,128)(2,1)S(1)}, u32[]{:S(2)}, u32[]{:S(2)}) collective-permute-start(bf16[256,128]{1,0:T(8,128)(2,1)S(1)} %get-tuple-element.72), channel_id=1, source_target_pairs={{0,8},{4,12},{8,0},{12,4},{1,9},{5,13},{9,1},{13,5},{2,10},{6,14},... | collective-permute-start | bytes 196616 | tf_op jit(solution)/shard_map/ppermute | solution.py:390
  47.7 12.4 %copy-start.6 = (bf16[3,512,128]{2,1,0:T(8,128)(2,1)S(1)}, bf16[3,512,128]{2,1,0:T(8,128)(2,1)}, u32[]{:S(2)}) copy-start(bf16[3,512,128]{2,1,0:T(8,128)(2,1)} %copy-done.5) | copy-start | bytes 1179652
  47.7 8.8 %collective-permute-start.13 = (bf16[256,128]{1,0:T(8,128)(2,1)S(1)}, bf16[256,128]{1,0:T(8,128)(2,1)S(1)}, u32[]{:S(2)}, u32[]{:S(2)}) collective-permute-start(bf16[256,128]{1,0:T(8,128)(2,1)S(1)} %get-tuple-element.73), channel_id=1, source_target_pairs={{0,12},{4,0},{8,4},{12,8},{1,13},{5,1},{9,5},{13,9},{2,14},{6,2},{... | collective-permute-start | bytes 196616 | tf_op jit(solution)/shard_map/ppermute | solution.py:390
  49.1 10.1 %collective-permute-start.14 = (bf16[256,128]{1,0:T(8,128)(2,1)S(1)}, bf16[256,128]{1,0:T(8,128)(2,1)S(1)}, u32[]{:S(2)}, u32[]{:S(2)}) collective-permute-start(bf16[256,128]{1,0:T(8,128)(2,1)S(1)} %get-tuple-element.75), channel_id=1, source_target_pairs={{0,4},{4,8},{8,12},{12,0},{1,5},{5,9},{9,13},{13,1},{2,6},{6,10},{... | collective-permute-start | bytes 196616 | tf_op jit(solution)/shard_map/ppermute | solution.py:390
  50.8 9.3 %collective-permute-start.15 = (bf16[256,128]{1,0:T(8,128)(2,1)S(1)}, bf16[256,128]{1,0:T(8,128)(2,1)S(1)}, u32[]{:S(2)}, u32[]{:S(2)}) collective-permute-start(bf16[256,128]{1,0:T(8,128)(2,1)S(1)} %get-tuple-element.76), channel_id=1, source_target_pairs={{0,8},{4,12},{8,0},{12,4},{1,9},{5,13},{9,1},{13,5},{2,10},{6,14},... | collective-permute-start | bytes 196616 | tf_op jit(solution)/shard_map/ppermute | solution.py:390
  51.8 8.3 %collective-permute-start.16 = (bf16[256,128]{1,0:T(8,128)(2,1)S(1)}, bf16[256,128]{1,0:T(8,128)(2,1)S(1)}, u32[]{:S(2)}, u32[]{:S(2)}) collective-permute-start(bf16[256,128]{1,0:T(8,128)(2,1)S(1)} %get-tuple-element.77), channel_id=1, source_target_pairs={{0,12},{4,0},{8,4},{12,8},{1,13},{5,1},{9,5},{13,9},{2,14},{6,2},{... | collective-permute-start | bytes 196616 | tf_op jit(solution)/shard_map/ppermute | solution.py:390
  54.7 28.3 %collective-permute-start.2 = (bf16[4,512,128]{2,1,0:T(8,128)(2,1)S(1)}, bf16[4,512,128]{2,1,0:T(8,128)(2,1)S(1)}, u32[]{:S(2)}, u32[]{:S(2)}) collective-permute-start(bf16[4,512,128]{2,1,0:T(8,128)(2,1)S(1)} %get-tuple-element.59), channel_id=1, source_target_pairs={{0,4},{4,8},{1,5},{5,9},{2,6},{6,10},{3,7},{7,11},{16,20},{20,24},... | collective-permute-start | bytes 1572872 | tf_op jit(solution)/shard_map/ppermute | solution.py:390
  56.5 27.5 %collective-permute-start.3 = (bf16[4,512,128]{2,1,0:T(8,128)(2,1)S(1)}, bf16[4,512,128]{2,1,0:T(8,128)(2,1)S(1)}, u32[]{:S(2)}, u32[]{:S(2)}) collective-permute-start(bf16[4,512,128]{2,1,0:T(8,128)(2,1)S(1)} %get-tuple-element.60), channel_id=1, source_target_pairs={{0,8},{12,4},{1,9},{13,5},{2,10},{14,6},{3,11},{15,7},{16,24},{28,... | collective-permute-start | bytes 1572872 | tf_op jit(solution)/shard_map/ppermute | solution.py:390
  59.3 24.8 %collective-permute-start.4 = (bf16[4,512,128]{2,1,0:T(8,128)(2,1)S(1)}, bf16[4,512,128]{2,1,0:T(8,128)(2,1)S(1)}, u32[]{:S(2)}, u32[]{:S(2)}) collective-permute-start(bf16[4,512,128]{2,1,0:T(8,128)(2,1)S(1)} %get-tuple-element.61), channel_id=1, source_target_pairs={{8,4},{12,8},{9,5},{13,9},{10,6},{14,10},{11,7},{15,11},{24,20},{2... | collective-permute-start | bytes 1572872 | tf_op jit(solution)/shard_map/ppermute | solution.py:390
  78.8 13.8 %collective-permute-start.17 = (bf16[1552,128]{1,0:T(8,128)(2,1)S(1)}, bf16[1552,128]{1,0:T(8,128)(2,1)S(1)}, u32[]{:S(2)}, u32[]{:S(2)}) collective-permute-start(bf16[1552,128]{1,0:T(8,128)(2,1)S(1)} %get-tuple-element.79), channel_id=1, source_target_pairs={{0,12},{4,0},{8,4},{12,8},{1,13},{5,1},{9,5},{13,9},{2,14},{6,2},{... | collective-permute-start | bytes 1191944 | tf_op jit(solution)/shard_map/ppermute | solution.py:394
  83.0 34.7 %collective-permute-start.18 = (bf16[1552,128]{1,0:T(8,128)(2,1)S(1)}, bf16[1552,128]{1,0:T(8,128)(2,1)S(1)}, u32[]{:S(2)}, u32[]{:S(2)}) collective-permute-start(bf16[1552,128]{1,0:T(8,128)(2,1)S(1)} %get-tuple-element.80), channel_id=1, source_target_pairs={{0,8},{4,12},{8,0},{12,4},{1,9},{5,13},{9,1},{13,5},{2,10},{6,14},... | collective-permute-start | bytes 1191944 | tf_op jit(solution)/shard_map/ppermute | solution.py:394
  83.0 34.7 %collective-permute-start.19 = (bf16[1552,128]{1,0:T(8,128)(2,1)S(1)}, bf16[1552,128]{1,0:T(8,128)(2,1)S(1)}, u32[]{:S(2)}, u32[]{:S(2)}) collective-permute-start(bf16[1552,128]{1,0:T(8,128)(2,1)S(1)} %get-tuple-element.81), channel_id=1, source_target_pairs={{0,4},{4,8},{8,12},{12,0},{1,5},{5,9},{9,13},{13,1},{2,6},{6,10},{... | collective-permute-start | bytes 1191944 | tf_op jit(solution)/shard_map/ppermute | solution.py:394
  84.9 40.2 %collective-permute-start.5 = (bf16[1552,128]{1,0:T(8,128)(2,1)S(1)}, bf16[1552,128]{1,0:T(8,128)(2,1)S(1)}, u32[]{:S(2)}, u32[]{:S(2)}) collective-permute-start(bf16[1552,128]{1,0:T(8,128)(2,1)S(1)} %get-tuple-element.63), channel_id=1, source_target_pairs={{4,0},{8,4},{5,1},{9,5},{6,2},{10,6},{7,3},{11,7},{20,16},{24,20},... | collective-permute-start | bytes 1191944 | tf_op jit(solution)/shard_map/ppermute | solution.py:394
  86.2 47.3 %collective-permute-start.6 = (bf16[1552,128]{1,0:T(8,128)(2,1)S(1)}, bf16[1552,128]{1,0:T(8,128)(2,1)S(1)}, u32[]{:S(2)}, u32[]{:S(2)}) collective-permute-start(bf16[1552,128]{1,0:T(8,128)(2,1)S(1)} %get-tuple-element.64), channel_id=1, source_target_pairs={{4,12},{8,0},{5,13},{9,1},{6,14},{10,2},{7,15},{11,3},{20,28},{24,... | collective-permute-start | bytes 1191944 | tf_op jit(solution)/shard_map/ppermute | solution.py:394
  92.6 40.9 %collective-permute-start.7 = (bf16[1552,128]{1,0:T(8,128)(2,1)S(1)}, bf16[1552,128]{1,0:T(8,128)(2,1)S(1)}, u32[]{:S(2)}, u32[]{:S(2)}) collective-permute-start(bf16[1552,128]{1,0:T(8,128)(2,1)S(1)} %get-tuple-element.65), channel_id=1, source_target_pairs={{4,8},{8,12},{5,9},{9,13},{6,10},{10,14},{7,11},{11,15},{20,24},{2... | collective-permute-start | bytes 1191944 | tf_op jit(solution)/shard_map/ppermute | solution.py:394
where the time goes:
time: 137 us; the launch traced here: 136 us
  waiting for transfers between devices  61.4 us (45%)
  Pallas kernels  37.1 us (27%)
  starting transfers between devices  32.5 us (24%)
  local copies, waits for them, and re-layouts  3.1 us (2%)
    ppermute x6, waiting for transfers between devices, shift_back(): return lax.ppermute(arr, axis, [(s, (s - step) % size) for s in sources])  43.6 us
    ppermute x12, starting transfers between devices, shift(): return lax.ppermute(arr, axis, pairs)  21 us
    pallas_call x2, Pallas kernels, attend(): pl.pallas_call(functools.partial(attend_kernel, parts, tiles_dev), out_sh...  19.4 us
    ppermute x2, waiting for transfers between devices, by_heads(): other.append(lax.ppermute(piece, 'head', [(0, 1), (1, 0)]))  17.8 us
    ppermute x6, starting transfers between devices, shift_back(): return lax.ppermute(arr, axis, [(s, (s - step) % size) for s in sources])  8.54 us
    pallas_call x2, Pallas kernels, stage(): pl.pallas_call(functools.partial(stage_kernel, slots, kinds, chunks), out...  5.82 us
    pallas_call x2, Pallas kernels, project_rest(): pl.pallas_call(project_rest_kernel, out_shape=[jax.ShapeDtypeStruct((rows...  5.15 us
    pallas_call x2, Pallas kernels, unpack(): pl.pallas_call(functools.partial(unpack_kernel, parts, rows, count, fresh...  3.87 us
  transfers between devices with their start and end apart: 20, of which 6 were waited for; matrix products, arithmetic and copies ran while one was open for 0% of the time, Pallas kernels for 24%

commit v1 on v0

--- a/solution.py
+++ b/solution.py
@@ -420,18 +420,29 @@
         targets.append(list(range(first, first + size)))
     mask = allowed_tiles(key_list[0], key_count[0])
     all_heads = jnp.concatenate(heads)
+    hops = [1, 3, 2] if parts == 4 else list(range(1, parts))
     chunk_count = rows // TILE
     tensors = (query_states[0], key_states[0], value_states[0])
-    first, pieces = stage(heads[0], tensors, output_grad[0], range(1, parts), [0])
-    own, rest = stage(heads[0], tensors, output_grad[0], [0], range(1, chunk_count))
-    pieces = [*pieces, *rest]
     other = []
+    moved, pieces = stage(heads[0], tensors, output_grad[0], hops[:1], [0])
+    blocks = [None] * parts
+
+    def trade(piece):
+        other.append(lax.ppermute(piece, "head", [(0, 1), (1, 0)]))
+
+    def send_first(hop, slot):
+        blocks[hop] = shift(slot, "seq", hop, parts, targets[0])
+
+    trade(pieces[0])
+    send_first(hops[0], moved[0])
+    moved, _ = stage(heads[0], tensors, output_grad[0], hops[1:], [])
+    for hop, slot in zip(hops[1:], moved):
+        send_first(hop, slot)
+    moved, pieces = stage(heads[0], tensors, output_grad[0], [0], range(1, chunk_count))
+    blocks[0] = moved[0]
     for piece in pieces:
-        if other:
-            piece, _ = lax.optimization_barrier((piece, other[-1]))
-        other.append(lax.ppermute(piece, "head", [(0, 1), (1, 0)]))
+        trade(piece)
     side = side.astype(jnp.int32).reshape(1)
-    blocks = [*own] + [shift(first[i - 1], "seq", i, parts, targets[0]) for i in range(1, parts)]
     acc = project_own(side, output_grad[0], w_out)
     projected = [
         project_rest(all_heads, 1 - side, other[chunk], w_out, acc, chunk)
@@ -439,9 +450,10 @@
     ]
     chunks = []
     for slots in projected:
-        chunks += [slots[0]]
-        for i in range(1, parts):
-            chunks += [shift(slots[i], "seq", i, parts, targets[0])]
+        landed = [slots[0]] + [None] * (parts - 1)
+        for i in hops:
+            landed[i] = shift(slots[i], "seq", i, parts, targets[0])
+        chunks += landed
     before = None
     for k in range(len(rounds)):
         me_live = jnp.stack([me.astype(jnp.int32), lives[k][0]])
@@ -449,13 +461,13 @@
         if k + 1 < len(rounds):
             grads = [slot for slots in projected for slot in slots[(k + 1) * parts : (k + 2) * parts]]
             slots = pack(heads[k + 1], *tensors, grads)
-            blocks = [slots[0]]
-            for i in range(1, parts):
-                blocks += [shift(slots[i], "seq", i, parts, targets[k + 1])]
+            blocks = [slots[0]] + [None] * (parts - 1)
+            for i in [1, 3, 2]:
+                blocks[i] = shift(slots[i], "seq", i, parts, targets[k + 1])
             chunks = []
-        back = [done[0]] + [
-            shift_back(done[i], "seq", i, parts, targets[k]) for i in range(1, parts)
-        ]
+        back = [done[0]] + [None] * (parts - 1)
+        for i in [2, 1, 3]:
+            back[i] = shift_back(done[i], "seq", i, parts, targets[k])
         before = unpack(heads[k], lives[k], back, before, head_count, parts * rows * HD)
     query_grad, key_grad, value_grad, feats = before
     return query_grad[None], key_grad[None], value_grad[None], feats.transpose(1, 2, 0)

time: 137 us -> 140 us (1.022)
  waiting for transfers between devices: 61.4 us -> 65.4 us
  starting transfers between devices: 32.5 us -> 29 us
  Pallas kernels: 37.1 us -> 39.5 us
    ppermute x2, waiting for transfers between devices: 17.8 us -> 21.6 us  [trade(): other.append(lax.ppermute(piece, 'head', [(0, 1), (1, 0)]))]
    ppermute x12, starting transfers between devices: 21 us -> 18.4 us  [shift(): return lax.ppermute(arr, axis, pairs)]
    pallas_call x2 -> x3, Pallas kernels: 5.82 us -> 8.23 us  [stage(): pl.pallas_call(functools.partial(stage_kernel, slots, kinds, chunks), out...]
  transfers between devices with their start and end apart: 20 -> 20, of which waited for: 6 -> 6; matrix products, arithmetic and copies ran while one was open for 0% -> 0% of each run, Pallas kernels for 24% -> 25%
where the time goes in v1:
time: 140 us; the launch traced here: 138 us
  waiting for transfers between devices  65.4 us (47%)
  Pallas kernels  39.5 us (28%)
  starting transfers between devices  29 us (21%)
  local copies, waits for them, and re-layouts  3.11 us (2%)
    ppermute x6, waiting for transfers between devices, shift_back(): return lax.ppermute(arr, axis, [(s, (s - step) % size) for s in sources])  43.8 us
    ppermute x2, waiting for transfers between devices, trade(): other.append(lax.ppermute(piece, 'head', [(0, 1), (1, 0)]))  21.6 us
    pallas_call x2, Pallas kernels, attend(): pl.pallas_call(functools.partial(attend_kernel, parts, tiles_dev), out_sh...  19.4 us
    ppermute x12, starting transfers between devices, shift(): return lax.ppermute(arr, axis, pairs)  18.4 us
    ppermute x6, starting transfers between devices, shift_back(): return lax.ppermute(arr, axis, [(s, (s - step) % size) for s in sources])  8.55 us
    pallas_call x3, Pallas kernels, stage(): pl.pallas_call(functools.partial(stage_kernel, slots, kinds, chunks), out...  8.23 us
    pallas_call x2, Pallas kernels, project_rest(): pl.pallas_call(project_rest_kernel, out_shape=[jax.ShapeDtypeStruct((rows...  5.13 us
    pallas_call x2, Pallas kernels, unpack(): pl.pallas_call(functools.partial(unpack_kernel, parts, rows, count, fresh...  3.87 us
  transfers between devices with their start and end apart: 20, of which 6 were waited for; matrix products, arithmetic and copies ran while one was open for 0% of the time, Pallas kernels for 25%

profile of v1, /device:TPU:4, one launch (start us, length us, event | category | flops | bytes accessed | tf_op | source)
XLA Modules:
  0.0 138.4 jit_solution(10151118753959991109)
XLA Ops:
  0.7 2.7 %stage_inputs.5 = (bf16[3,512,128]{2,1,0:T(8,128)(2,1)}, bf16[3,512,128]{2,1,0:T(8,128)(2,1)}) custom-call(s32[4]{0:T(128)S(1)} %broadcast_clamp_fusion.heads_ref, bf16[512,768]{1,0:T(8,128)(2,1)} %bitcast.20, bf16[512,768]{1,0:T(8,128)(2,1)} %bitcast.24, bf16[512,768]{1,0:T(8,128)(2,1)} %bitcast.28, bf16[512,1536]{1,0:T(8,128)(2,1)} %bitcast.16), custom_call_target="tpu_custom_call" | custom-call | bytes 1572864 | tf_op jit(solution)/shard_map/stage_inputs/pallas_call | solution.py:57
  3.4 2.7 %collective-permute-start.9 = (bf16[3,512,128]{2,1,0:T(8,128)(2,1)}, bf16[3,512,128]{2,1,0:T(8,128)(2,1)S(1)}, u32[]{:S(2)}, u32[]{:S(2)}) collective-permute-start(bf16[3,512,128]{2,1,0:T(8,128)(2,1)} %get-tuple-element.66), channel_id=1, source_target_pairs={{0,8},{4,12},{8,0},{12,4},{1,9},{5,13},{9,1},{13,5},{2,10},{6,14},... | collective-permute-start | bytes 1179656 | tf_op jit(solution)/shard_map/ppermute | solution.py:390
  6.0 1.3 collective-permute-start.10
  7.4 2.7 %stage_inputs.4 = (bf16[3,512,128]{2,1,0:T(8,128)(2,1)S(1)}, bf16[256,1536]{1,0:T(8,128)(2,1)}) custom-call(s32[4]{0:T(128)S(1)} %broadcast_clamp_fusion.heads_ref, bf16[512,768]{1,0:T(8,128)(2,1)} %bitcast.21, bf16[512,768]{1,0:T(8,128)(2,1)} %bitcast.25, bf16[512,768]{1,0:T(8,128)(2,1)} %bitcast.29, bf16[512,1536]{1,0:T(8,128)(2,1)} %bitcast.17), custom_call_target="tpu_custom_call" | custom-call | bytes 2359296 | tf_op jit(solution)/shard_map/stage_inputs/pallas_call | solution.py:57
  10.1 0.0 copy-start.5
  10.1 0.7 copy-done.5
  10.8 1.5 %collective-permute-start.1 = (bf16[256,1536]{1,0:T(8,128)(2,1)}, bf16[256,1536]{1,0:T(8,128)(2,1)}, u32[]{:S(2)}, u32[]{:S(2)}) collective-permute-start(bf16[256,1536]{1,0:T(8,128)(2,1)} %get-tuple-element.51), channel_id=1, source_target_pairs={{0,2},{2,0},{1,3},{3,1},{4,6},{6,4},{5,7},{7,5},{8,10},{10,8},{9,1... | collective-permute-start | bytes 2359304 | tf_op jit(solution)/shard_map/ppermute | solution.py:431
  12.3 2.8 %stage_inputs.3 = (bf16[3,512,128]{2,1,0:T(8,128)(2,1)}, bf16[256,1536]{1,0:T(8,128)(2,1)}) custom-call(s32[4]{0:T(128)S(1)} %broadcast_clamp_fusion.heads_ref, bf16[512,768]{1,0:T(8,128)(2,1)} %bitcast.22, bf16[512,768]{1,0:T(8,128)(2,1)} %bitcast.26, bf16[512,768]{1,0:T(8,128)(2,1)} %bitcast.30, bf16[512,1536]{1,0:T(8,128)(2,1)} %bitcast.18), custom_call_target="tpu_custom_call" | custom-call | bytes 2359296 | tf_op jit(solution)/shard_map/stage_inputs/pallas_call | solution.py:57
  15.2 0.7 collective-permute-start.8
  15.9 0.5 collective-permute-start
  16.4 0.0 copy-done.1
  16.5 0.0 copy-start
  16.5 2.3 %copy-done = bf16[768,3072]{1,0:T(8,128)(2,1)S(1)} copy-done((bf16[768,3072]{1,0:T(8,128)(2,1)S(1)}, bf16[768,3072]{1,0:T(8,128)(2,1)}, u32[]{:S(2)}) %copy-start) | copy-done | bytes 4718616
  18.8 2.0 %project_own.1.acc_ref = f32[3,512,256]{2,1,0:T(8,128)S(1)} custom-call(s32[1]{0:T(128)} %bitcast.6.src_ref, bf16[512,1536]{1,0:T(8,128)(2,1)S(1)} %bitcast.19, bf16[768,3072]{1,0:T(8,128)(2,1)S(1)} %copy-done), custom_call_target="tpu_custom_call" | custom-call | flops 1207959552 | bytes 5505024 | tf_op jit(solution)/shard_map/project_own/pallas_call | solution.py:112
  20.9 0.0 copy-done.8
  20.9 0.1 iota_compare_fusion.1
  20.9 0.1 pad_add_fusion.1.heads_ref
  21.0 0.0 copy-done.7
  21.0 0.1 fusion.1
  21.1 10.4 %collective-permute-done.1.grad_ref = bf16[256,1536]{1,0:T(8,128)(2,1)} collective-permute-done((bf16[256,1536]{1,0:T(8,128)(2,1)}, bf16[256,1536]{1,0:T(8,128)(2,1)}, u32[]{:S(2)}, u32[]{:S(2)}) %collective-permute-start.1) | collective-permute-done | bytes 786464 | tf_op jit(solution)/shard_map/ppermute | solution.py:431
  31.6 0.0 slice-done
  31.6 3.1 %project_rest.3 = (bf16[256,128]{1,0:T(8,128)(2,1)S(1)}, bf16[256,128]{1,0:T(8,128)(2,1)S(1)}, bf16[256,128]{1,0:T(8,128)(2,1)S(1)}, bf16[256,128]{1,0:T(8,128)(...) custom-call(s32[8]{0:T(128)S(1)} %pad_add_fusion.1.heads_ref, ...), custom_call_target="tpu_custom_call" | custom-call | flops 603979776 | bytes 4325376 | tf_op jit(solution)/shard_map/project_rest/pallas_call | solution.py:152
  34.7 0.7 collective-permute-start.14
  35.4 11.2 %collective-permute-done.grad_ref = bf16[256,1536]{1,0:T(8,128)(2,1)S(1)} collective-permute-done((bf16[256,1536]{1,0:T(8,128)(2,1)}, bf16[256,1536]{1,0:T(8,128)(2,1)S(1)}, u32[]{:S(2)}, u32[]{:S(2)}) %collective-permute-start) | collective-permute-done | bytes 786464 | tf_op jit(solution)/shard_map/ppermute | solution.py:431
  46.6 1.7 %collective-permute-start.15 = (bf16[256,128]{1,0:T(8,128)(2,1)S(1)}, bf16[256,128]{1,0:T(8,128)(2,1)S(1)}, u32[]{:S(2)}, u32[]{:S(2)}) collective-permute-start(bf16[256,128]{1,0:T(8,128)(2,1)S(1)} %get-tuple-element.74), channel_id=1, source_target_pairs={{0,8},{4,12},{8,0},{12,4},{1,9},{5,13},{9,1},{13,5},{2,10},{6,14},... | collective-permute-start | bytes 196616 | tf_op jit(solution)/shard_map/ppermute | solution.py:390
  48.3 2.0 %project_rest.2 = (bf16[256,128]{1,0:T(8,128)(2,1)S(1)}, bf16[256,128]{1,0:T(8,128)(2,1)S(1)}, bf16[256,128]{1,0:T(8,128)(2,1)S(1)}, bf16[256,128]{1,0:T(8,128)(...) custom-call(s32[8]{0:T(128)S(1)} %pad_add_fusion.1.heads_ref, ...), custom_call_target="tpu_custom_call" | custom-call | flops 603979776 | bytes 4325376 | tf_op jit(solution)/shard_map/project_rest/pallas_call | solution.py:152
  50.4 0.0 collective-permute-done.9.refs_2_
  50.4 1.4 %collective-permute-start.16 = (bf16[256,128]{1,0:T(8,128)(2,1)S(1)}, bf16[256,128]{1,0:T(8,128)(2,1)S(1)}, u32[]{:S(2)}, u32[]{:S(2)}) collective-permute-start(bf16[256,128]{1,0:T(8,128)(2,1)S(1)} %get-tuple-element.75), channel_id=1, source_target_pairs={{0,12},{4,0},{8,4},{12,8},{1,13},{5,1},{9,5},{13,9},{2,14},{6,2},{... | collective-permute-start | bytes 196616 | tf_op jit(solution)/shard_map/ppermute | solution.py:390
  51.8 0.0 collective-permute-done.10.refs_3_
  51.8 0.7 collective-permute-start.11
  52.4 0.1 pad_add_fusion.me_ref
  52.6 0.8 pack_heads.1
  53.4 0.0 collective-permute-done.8.refs_1_
  53.4 1.3 collective-permute-start.12
  54.7 0.0 collective-permute-done.14.refs_9_
  54.7 2.0 %collective-permute-start.13 = (bf16[256,128]{1,0:T(8,128)(2,1)S(1)}, bf16[256,128]{1,0:T(8,128)(2,1)S(1)}, u32[]{:S(2)}, u32[]{:S(2)}) collective-permute-start(bf16[256,128]{1,0:T(8,128)(2,1)S(1)} %get-tuple-element.71), channel_id=1, source_target_pairs={{0,12},{4,0},{8,4},{12,8},{1,13},{5,1},{9,5},{13,9},{2,14},{6,2},{... | collective-permute-start | bytes 196616 | tf_op jit(solution)/shard_map/ppermute | solution.py:390
  56.7 0.0 collective-permute-done.15.refs_10_
  56.7 2.4 %collective-permute-start.2 = (bf16[4,512,128]{2,1,0:T(8,128)(2,1)S(1)}, bf16[4,512,128]{2,1,0:T(8,128)(2,1)S(1)}, u32[]{:S(2)}, u32[]{:S(2)}) collective-permute-start(bf16[4,512,128]{2,1,0:T(8,128)(2,1)S(1)} %get-tuple-element.57), channel_id=1, source_target_pairs={{0,4},{4,8},{1,5},{5,9},{2,6},{6,10},{3,7},{7,11},{16,20},{20,24},... | collective-permute-start | bytes 1572872 | tf_op jit(solution)/shard_map/ppermute | solution.py:390
  59.2 0.0 collective-permute-done.16.refs_11_
  59.2 2.7 %collective-permute-start.3 = (bf16[4,512,128]{2,1,0:T(8,128)(2,1)S(1)}, bf16[4,512,128]{2,1,0:T(8,128)(2,1)S(1)}, u32[]{:S(2)}, u32[]{:S(2)}) collective-permute-start(bf16[4,512,128]{2,1,0:T(8,128)(2,1)S(1)} %get-tuple-element.58), channel_id=1, source_target_pairs={{0,8},{12,4},{1,9},{13,5},{2,10},{14,6},{3,11},{15,7},{16,24},{28,... | collective-permute-start | bytes 1572872 | tf_op jit(solution)/shard_map/ppermute | solution.py:390
  61.9 0.0 collective-permute-done.11.refs_5_
  61.9 0.7 collective-permute-start.4
  62.6 0.1 pad_add_fusion.2.me_ref
  62.7 0.0 collective-permute-done.12.refs_6_
  62.7 0.0 collective-permute-done.13.refs_7_
  62.8 18.6 %attend_head.3 = (bf16[1552,128]{1,0:T(8,128)(2,1)S(1)}, bf16[1552,128]{1,0:T(8,128)(2,1)S(1)}, bf16[1552,128]{1,0:T(8,128)(2,1)S(1)}, bf16[1552,128]{1,0:T(8,128)(2,1)S(1)}) custom-call(s32[2]{0:T(128)S(1)} %pad_add_fusion.2.me_ref, s32[8,8]{1,0:T(8,128)S(1)} %convert_element_type.10.mask_ref, bf16[3,512,128]{2,1,0:T(8,128)(2,1)S(1)} %copy-done.6, ...), custom_call_target="tpu_custom_call" | custom-call | flops 5368709120 | bytes 3670016 | tf_op jit(solution)/shard_map/attend_head/pallas_call | solution.py:290
  81.4 4.2 %collective-permute-start.17 = (bf16[1552,128]{1,0:T(8,128)(2,1)S(1)}, bf16[1552,128]{1,0:T(8,128)(2,1)S(1)}, u32[]{:S(2)}, u32[]{:S(2)}) collective-permute-start(bf16[1552,128]{1,0:T(8,128)(2,1)S(1)} %get-tuple-element.77), channel_id=1, source_target_pairs={{0,12},{4,0},{8,4},{12,8},{1,13},{5,1},{9,5},{13,9},{2,14},{6,2},{... | collective-permute-start | bytes 1191944 | tf_op jit(solution)/shard_map/ppermute | solution.py:394
  85.6 0.0 collective-permute-start.18
  85.6 0.0 collective-permute-done.2.refs_1_
  85.6 1.1 collective-permute-start.19
  86.7 0.0 collective-permute-done.3.refs_2_
  86.7 0.0 collective-permute-done.4.refs_3_
  86.7 0.8 attend_head.2
  87.5 1.3 collective-permute-start.5
  88.8 1.3 collective-permute-start.6
  90.1 5.1 %collective-permute-done.17.refs_1_ = bf16[1552,128]{1,0:T(8,128)(2,1)S(1)} collective-permute-done((bf16[1552,128]{1,0:T(8,128)(2,1)S(1)}, bf16[1552,128]{1,0:T(8,128)(2,1)S(1)}, u32[]{:S(2)}, u32[]{:S(2)}) %collective-permute-start.17) | collective-permute-done | bytes 397344 | tf_op jit(solution)/shard_map/ppermute | solution.py:394
  95.2 0.7 collective-permute-start.7
  95.9 24.4 %collective-permute-done.18.refs_2_ = bf16[1552,128]{1,0:T(8,128)(2,1)S(1)} collective-permute-done((bf16[1552,128]{1,0:T(8,128)(2,1)S(1)}, bf16[1552,128]{1,0:T(8,128)(2,1)S(1)}, u32[]{:S(2)}, u32[]{:S(2)}) %collective-permute-start.18) | collective-permute-done | bytes 397344 | tf_op jit(solution)/shard_map/ppermute | solution.py:394
  120.3 0.0 collective-permute-done.19.refs_3_
  120.3 1.8 %unpack_heads.2 = (bf16[512,768]{1,0:T(8,128)(2,1)}, bf16[512,768]{1,0:T(8,128)(2,1)}, bf16[512,768]{1,0:T(8,128)(2,1)}, f32[3,1,6]{2,1,0:T(1,128)S(1)}) custom-call(s32[4]{0:T(128)S(1)} %broadcast_clamp_fusion.heads_ref, s32[4]{0:T(128)S(1)} %and_convert_fusion.live_ref, bf16[1552,128]{1,0:T(8,128)(2,1)S(1)} %get-tuple-element.76.refs_0_, ...), custom_call_target="tpu_custom_call" | custom-call | bytes 3145728 | tf_op jit(solution)/shard_map/unpack_heads/pallas_call | solution.py:373
  122.1 5.8 %collective-permute-done.5.refs_1_ = bf16[1552,128]{1,0:T(8,128)(2,1)S(1)} collective-permute-done((bf16[1552,128]{1,0:T(8,128)(2,1)S(1)}, bf16[1552,128]{1,0:T(8,128)(2,1)S(1)}, u32[]{:S(2)}, u32[]{:S(2)}) %collective-permute-start.5) | collective-permute-done | bytes 397344 | tf_op jit(solution)/shard_map/ppermute | solution.py:394
  127.8 8.5 %collective-permute-done.6.refs_2_ = bf16[1552,128]{1,0:T(8,128)(2,1)S(1)} collective-permute-done((bf16[1552,128]{1,0:T(8,128)(2,1)S(1)}, bf16[1552,128]{1,0:T(8,128)(2,1)S(1)}, u32[]{:S(2)}, u32[]{:S(2)}) %collective-permute-start.6) | collective-permute-done | bytes 397344 | tf_op jit(solution)/shard_map/ppermute | solution.py:394
  136.3 0.0 collective-permute-done.7.refs_3_
  136.3 2.1 %unpack_heads.3 = (bf16[512,768]{1,0:T(8,128)(2,1)}, bf16[512,768]{1,0:T(8,128)(2,1)}, bf16[512,768]{1,0:T(8,128)(2,1)}, f32[3,1,6]{2,1,0:T(1,128)}) custom-call(s32[4]{0:T(128)S(1)} %clamp_add_fusion.heads_ref, s32[4]{0:T(128)S(1)} %and_convert_fusion.1.live_ref, ...), custom_call_target="tpu_custom_call", output_to_operand_aliasing={{0}: (6, {}), {1}: (7, {}), {2}: (8, {})} | custom-call | bytes 3145728 | tf_op jit(solution)/shard_map/unpack_heads/pallas_call | solution.py:373
  (20 shorter events, 0.1 us)
Async XLA Ops:
  3.4 47.0 %collective-permute-start.9 = (bf16[3,512,128]{2,1,0:T(8,128)(2,1)}, bf16[3,512,128]{2,1,0:T(8,128)(2,1)S(1)}, u32[]{:S(2)}, u32[]{:S(2)}) collective-permute-start(bf16[3,512,128]{2,1,0:T(8,128)(2,1)} %get-tuple-element.66), channel_id=1, source_target_pairs={{0,8},{4,12},{8,0},{12,4},{1,9},{5,13},{9,1},{13,5},{2,10},{6,14},... | collective-permute-start | bytes 1179656 | tf_op jit(solution)/shard_map/ppermute | solution.py:390
  6.0 45.7 %collective-permute-start.10 = (bf16[3,512,128]{2,1,0:T(8,128)(2,1)}, bf16[3,512,128]{2,1,0:T(8,128)(2,1)}, u32[]{:S(2)}, u32[]{:S(2)}) collective-permute-start(bf16[3,512,128]{2,1,0:T(8,128)(2,1)} %get-tuple-element.67), channel_id=1, source_target_pairs={{0,12},{4,0},{8,4},{12,8},{1,13},{5,1},{9,5},{13,9},{2,14},{6,2},{... | collective-permute-start | bytes 1179656 | tf_op jit(solution)/shard_map/ppermute | solution.py:390
  10.1 0.8 copy-start.5
  10.8 5.6 %copy-start.1 = (bf16[1,512,1536]{2,1,0:T(8,128)(2,1)S(1)}, bf16[1,512,1536]{2,1,0:T(8,128)(2,1)}, u32[]{:S(2)}) copy-start(bf16[1,512,1536]{2,1,0:T(8,128)(2,1)} %param.10) | copy-start | bytes 4718596
  10.8 20.7 %collective-permute-start.1 = (bf16[256,1536]{1,0:T(8,128)(2,1)}, bf16[256,1536]{1,0:T(8,128)(2,1)}, u32[]{:S(2)}, u32[]{:S(2)}) collective-permute-start(bf16[256,1536]{1,0:T(8,128)(2,1)} %get-tuple-element.51), channel_id=1, source_target_pairs={{0,2},{2,0},{1,3},{3,1},{4,6},{6,4},{5,7},{7,5},{8,10},{10,8},{9,1... | collective-permute-start | bytes 2359304 | tf_op jit(solution)/shard_map/ppermute | solution.py:431
  12.3 19.2 %slice-start = ((s8[4718592]{0:T(1024)(128)(4,1)}), s8[524288]{0:T(1024)(128)(4,1)S(1)}, s32[]{:S(2)}) async-start(s8[4718592]{0:T(1024)(128)(4,1)} %bitcast.14), calls=%async_computation | async-start | bytes 1048576
  15.2 38.3 %collective-permute-start.8 = (bf16[3,512,128]{2,1,0:T(8,128)(2,1)}, bf16[3,512,128]{2,1,0:T(8,128)(2,1)}, u32[]{:S(2)}, u32[]{:S(2)}) collective-permute-start(bf16[3,512,128]{2,1,0:T(8,128)(2,1)} %get-tuple-element.65), channel_id=1, source_target_pairs={{0,4},{4,8},{8,12},{12,0},{1,5},{5,9},{9,13},{13,1},{2,6},{6,10},{... | collective-permute-start | bytes 1179656 | tf_op jit(solution)/shard_map/ppermute | solution.py:390
  15.9 30.8 %collective-permute-start = (bf16[256,1536]{1,0:T(8,128)(2,1)}, bf16[256,1536]{1,0:T(8,128)(2,1)S(1)}, u32[]{:S(2)}, u32[]{:S(2)}) collective-permute-start(bf16[256,1536]{1,0:T(8,128)(2,1)} %get-tuple-element.46), channel_id=1, source_target_pairs={{0,2},{2,0},{1,3},{3,1},{4,6},{6,4},{5,7},{7,5},{8,10},{10,8},{9,1... | collective-permute-start | bytes 2359304 | tf_op jit(solution)/shard_map/ppermute | solution.py:431
  16.5 2.3 %copy-start = (bf16[768,3072]{1,0:T(8,128)(2,1)S(1)}, bf16[768,3072]{1,0:T(8,128)(2,1)}, u32[]{:S(2)}) copy-start(bf16[768,3072]{1,0:T(8,128)(2,1)} %w_ref.5) | copy-start | bytes 14155780
  18.8 2.1 %copy-start.8 = (s32[1,8]{1,0:T(1,128)S(1)}, s32[1,8]{1,0:T(1,128)}, u32[]{:S(2)}) copy-start(s32[1,8]{1,0:T(1,128)} %param.13) | copy-start | bytes 100
  18.8 2.2 %copy-start.7 = (s32[1,8,8]{2,1,0:T(8,128)S(1)}, s32[1,8,8]{2,1,0:T(8,128)}, u32[]{:S(2)}) copy-start(s32[1,8,8]{2,1,0:T(8,128)} %param.12) | copy-start | bytes 772
  18.8 12.8 %slice-start.1 = ((s8[4718592]{0:T(1024)(128)(4,1)}), s8[4194304]{0:T(1024)(128)(4,1)S(1)}, s32[]{:S(2)}) async-start(s8[4718592]{0:T(1024)(128)(4,1)} %bitcast.14), calls=%async_computation.1 | async-start | bytes 8388608
  34.7 20.0 %collective-permute-start.14 = (bf16[256,128]{1,0:T(8,128)(2,1)S(1)}, bf16[256,128]{1,0:T(8,128)(2,1)S(1)}, u32[]{:S(2)}, u32[]{:S(2)}) collective-permute-start(bf16[256,128]{1,0:T(8,128)(2,1)S(1)} %get-tuple-element.73), channel_id=1, source_target_pairs={{0,4},{4,8},{8,12},{12,0},{1,5},{5,9},{9,13},{13,1},{2,6},{6,10},{... | collective-permute-start | bytes 196616 | tf_op jit(solution)/shard_map/ppermute | solution.py:390
  46.6 5.9 %copy-start.2 = (bf16[1,512,768]{2,1,0:T(8,128)(2,1)S(1)}, bf16[1,512,768]{2,1,0:T(8,128)(2,1)}, u32[]{:S(2)}) copy-start(bf16[1,512,768]{2,1,0:T(8,128)(2,1)} %param.7) | copy-start | bytes 2359300
  46.6 5.9 %copy-start.3 = (bf16[1,512,768]{2,1,0:T(8,128)(2,1)S(1)}, bf16[1,512,768]{2,1,0:T(8,128)(2,1)}, u32[]{:S(2)}) copy-start(bf16[1,512,768]{2,1,0:T(8,128)(2,1)} %param.8) | copy-start | bytes 2359300
  46.6 5.9 %copy-start.4 = (bf16[1,512,768]{2,1,0:T(8,128)(2,1)S(1)}, bf16[1,512,768]{2,1,0:T(8,128)(2,1)}, u32[]{:S(2)}) copy-start(bf16[1,512,768]{2,1,0:T(8,128)(2,1)} %param.9) | copy-start | bytes 2359300
  46.6 10.1 %collective-permute-start.15 = (bf16[256,128]{1,0:T(8,128)(2,1)S(1)}, bf16[256,128]{1,0:T(8,128)(2,1)S(1)}, u32[]{:S(2)}, u32[]{:S(2)}) collective-permute-start(bf16[256,128]{1,0:T(8,128)(2,1)S(1)} %get-tuple-element.74), channel_id=1, source_target_pairs={{0,8},{4,12},{8,0},{12,4},{1,9},{5,13},{9,1},{13,5},{2,10},{6,14},... | collective-permute-start | bytes 196616 | tf_op jit(solution)/shard_map/ppermute | solution.py:390
  50.3 12.4 %copy-start.6 = (bf16[3,512,128]{2,1,0:T(8,128)(2,1)S(1)}, bf16[3,512,128]{2,1,0:T(8,128)(2,1)}, u32[]{:S(2)}) copy-start(bf16[3,512,128]{2,1,0:T(8,128)(2,1)} %copy-done.5) | copy-start | bytes 1179652
  50.4 8.8 %collective-permute-start.16 = (bf16[256,128]{1,0:T(8,128)(2,1)S(1)}, bf16[256,128]{1,0:T(8,128)(2,1)S(1)}, u32[]{:S(2)}, u32[]{:S(2)}) collective-permute-start(bf16[256,128]{1,0:T(8,128)(2,1)S(1)} %get-tuple-element.75), channel_id=1, source_target_pairs={{0,12},{4,0},{8,4},{12,8},{1,13},{5,1},{9,5},{13,9},{2,14},{6,2},{... | collective-permute-start | bytes 196616 | tf_op jit(solution)/shard_map/ppermute | solution.py:390
  51.8 10.1 %collective-permute-start.11 = (bf16[256,128]{1,0:T(8,128)(2,1)S(1)}, bf16[256,128]{1,0:T(8,128)(2,1)S(1)}, u32[]{:S(2)}, u32[]{:S(2)}) collective-permute-start(bf16[256,128]{1,0:T(8,128)(2,1)S(1)} %get-tuple-element.69), channel_id=1, source_target_pairs={{0,4},{4,8},{8,12},{12,0},{1,5},{5,9},{9,13},{13,1},{2,6},{6,10},{... | collective-permute-start | bytes 196616 | tf_op jit(solution)/shard_map/ppermute | solution.py:390
  53.4 9.3 %collective-permute-start.12 = (bf16[256,128]{1,0:T(8,128)(2,1)S(1)}, bf16[256,128]{1,0:T(8,128)(2,1)S(1)}, u32[]{:S(2)}, u32[]{:S(2)}) collective-permute-start(bf16[256,128]{1,0:T(8,128)(2,1)S(1)} %get-tuple-element.70), channel_id=1, source_target_pairs={{0,8},{4,12},{8,0},{12,4},{1,9},{5,13},{9,1},{13,5},{2,10},{6,14},... | collective-permute-start | bytes 196616 | tf_op jit(solution)/shard_map/ppermute | solution.py:390
  54.7 8.0 %collective-permute-start.13 = (bf16[256,128]{1,0:T(8,128)(2,1)S(1)}, bf16[256,128]{1,0:T(8,128)(2,1)S(1)}, u32[]{:S(2)}, u32[]{:S(2)}) collective-permute-start(bf16[256,128]{1,0:T(8,128)(2,1)S(1)} %get-tuple-element.71), channel_id=1, source_target_pairs={{0,12},{4,0},{8,4},{12,8},{1,13},{5,1},{9,5},{13,9},{2,14},{6,2},{... | collective-permute-start | bytes 196616 | tf_op jit(solution)/shard_map/ppermute | solution.py:390
  56.7 28.9 %collective-permute-start.2 = (bf16[4,512,128]{2,1,0:T(8,128)(2,1)S(1)}, bf16[4,512,128]{2,1,0:T(8,128)(2,1)S(1)}, u32[]{:S(2)}, u32[]{:S(2)}) collective-permute-start(bf16[4,512,128]{2,1,0:T(8,128)(2,1)S(1)} %get-tuple-element.57), channel_id=1, source_target_pairs={{0,4},{4,8},{1,5},{5,9},{2,6},{6,10},{3,7},{7,11},{16,20},{20,24},... | collective-permute-start | bytes 1572872 | tf_op jit(solution)/shard_map/ppermute | solution.py:390
  59.2 27.5 %collective-permute-start.3 = (bf16[4,512,128]{2,1,0:T(8,128)(2,1)S(1)}, bf16[4,512,128]{2,1,0:T(8,128)(2,1)S(1)}, u32[]{:S(2)}, u32[]{:S(2)}) collective-permute-start(bf16[4,512,128]{2,1,0:T(8,128)(2,1)S(1)} %get-tuple-element.58), channel_id=1, source_target_pairs={{0,8},{12,4},{1,9},{13,5},{2,10},{14,6},{3,11},{15,7},{16,24},{28,... | collective-permute-start | bytes 1572872 | tf_op jit(solution)/shard_map/ppermute | solution.py:390
  61.9 24.8 %collective-permute-start.4 = (bf16[4,512,128]{2,1,0:T(8,128)(2,1)S(1)}, bf16[4,512,128]{2,1,0:T(8,128)(2,1)S(1)}, u32[]{:S(2)}, u32[]{:S(2)}) collective-permute-start(bf16[4,512,128]{2,1,0:T(8,128)(2,1)S(1)} %get-tuple-element.59), channel_id=1, source_target_pairs={{8,4},{12,8},{9,5},{13,9},{10,6},{14,10},{11,7},{15,11},{24,20},{2... | collective-permute-start | bytes 1572872 | tf_op jit(solution)/shard_map/ppermute | solution.py:390
  81.4 13.8 %collective-permute-start.17 = (bf16[1552,128]{1,0:T(8,128)(2,1)S(1)}, bf16[1552,128]{1,0:T(8,128)(2,1)S(1)}, u32[]{:S(2)}, u32[]{:S(2)}) collective-permute-start(bf16[1552,128]{1,0:T(8,128)(2,1)S(1)} %get-tuple-element.77), channel_id=1, source_target_pairs={{0,12},{4,0},{8,4},{12,8},{1,13},{5,1},{9,5},{13,9},{2,14},{6,2},{... | collective-permute-start | bytes 1191944 | tf_op jit(solution)/shard_map/ppermute | solution.py:394
  85.6 34.7 %collective-permute-start.18 = (bf16[1552,128]{1,0:T(8,128)(2,1)S(1)}, bf16[1552,128]{1,0:T(8,128)(2,1)S(1)}, u32[]{:S(2)}, u32[]{:S(2)}) collective-permute-start(bf16[1552,128]{1,0:T(8,128)(2,1)S(1)} %get-tuple-element.78), channel_id=1, source_target_pairs={{0,8},{4,12},{8,0},{12,4},{1,9},{5,13},{9,1},{13,5},{2,10},{6,14},... | collective-permute-start | bytes 1191944 | tf_op jit(solution)/shard_map/ppermute | solution.py:394
  85.6 34.7 %collective-permute-start.19 = (bf16[1552,128]{1,0:T(8,128)(2,1)S(1)}, bf16[1552,128]{1,0:T(8,128)(2,1)S(1)}, u32[]{:S(2)}, u32[]{:S(2)}) collective-permute-start(bf16[1552,128]{1,0:T(8,128)(2,1)S(1)} %get-tuple-element.79), channel_id=1, source_target_pairs={{0,4},{4,8},{8,12},{12,0},{1,5},{5,9},{9,13},{13,1},{2,6},{6,10},{... | collective-permute-start | bytes 1191944 | tf_op jit(solution)/shard_map/ppermute | solution.py:394
  87.5 40.4 %collective-permute-start.5 = (bf16[1552,128]{1,0:T(8,128)(2,1)S(1)}, bf16[1552,128]{1,0:T(8,128)(2,1)S(1)}, u32[]{:S(2)}, u32[]{:S(2)}) collective-permute-start(bf16[1552,128]{1,0:T(8,128)(2,1)S(1)} %get-tuple-element.61), channel_id=1, source_target_pairs={{4,0},{8,4},{5,1},{9,5},{6,2},{10,6},{7,3},{11,7},{20,16},{24,20},... | collective-permute-start | bytes 1191944 | tf_op jit(solution)/shard_map/ppermute | solution.py:394
  88.8 47.5 %collective-permute-start.6 = (bf16[1552,128]{1,0:T(8,128)(2,1)S(1)}, bf16[1552,128]{1,0:T(8,128)(2,1)S(1)}, u32[]{:S(2)}, u32[]{:S(2)}) collective-permute-start(bf16[1552,128]{1,0:T(8,128)(2,1)S(1)} %get-tuple-element.62), channel_id=1, source_target_pairs={{4,12},{8,0},{5,13},{9,1},{6,14},{10,2},{7,15},{11,3},{20,28},{24,... | collective-permute-start | bytes 1191944 | tf_op jit(solution)/shard_map/ppermute | solution.py:394
  95.2 41.1 %collective-permute-start.7 = (bf16[1552,128]{1,0:T(8,128)(2,1)S(1)}, bf16[1552,128]{1,0:T(8,128)(2,1)S(1)}, u32[]{:S(2)}, u32[]{:S(2)}) collective-permute-start(bf16[1552,128]{1,0:T(8,128)(2,1)S(1)} %get-tuple-element.63), channel_id=1, source_target_pairs={{4,8},{8,12},{5,9},{9,13},{6,10},{10,14},{7,11},{11,15},{20,24},{2... | collective-permute-start | bytes 1191944 | tf_op jit(solution)/shard_map/ppermute | solution.py:394
